TPU v7x, 256 devices: a whole 4x4x8 slice. The times are simulated.
256 devices in a mesh: chan: 32 (over y, z), bins: 8 (over x, core).
Axes of the slice: x: 4, y: 4, z: 8, core: 2. Of those that a mesh axis runs over, the one named last changes fastest.
Arguments:
- effects: bfloat16 [256, 16384, 256], P('chan', 'bins'), may hold values from -0.19921875 to 0.19921875
- nominal: float32 [256, 16384], P('chan', 'bins'), may hold values from 0.2 to 5
- observed: int32 [256, 16384], P('chan', 'bins'), may hold values from 0 to 7
- mc_variance: float32 [256, 16384], P('chan', 'bins'), may hold values from 0.002 to 0.5
- theta: float32 [8192], replicated, may hold values from -4 to 4
- nuisance_index: int32 [256, 256], replicated, may hold values from 0 to 8191, as said below
- bin_counts: int32 [256], P('chan'), may hold values from 1 to 16384, 2097152 in all
- tile_owner: int32 [256], replicated, may hold values from 0 to 255, each once
Outputs:
- hessian_tiles: float32 [256, 512, 512], P(('chan', 'bins'))
- gradient: float32 [8192], P(('chan', 'bins'))
Inputs may be any that keep to these rules, and one draw needn't show every extreme that they name: `nuisance_index`: each channel's list is 2 runs of 128 consecutive nuisances, each run starting at a multiple of 128, the runs distinct and in increasing order. Bins at positions bin_counts[c] and beyond of channel c carry no data. `tile_owner`: every tile number appears exactly once.
All inputs are finite; a program needn't handle non-finite values. No bound on the sum of `bin_counts` on one device may be relied on, other than what follows from the above.
Results may differ from a plain program's by a relative error of at most 0.0029.
Values sent between devices are 32-bit elements; how exact they have to be, the bound alone decides.
No kernel may reach another device: no remote copies, remote signals or barrier semaphores. Data moves between devices by JAX's collectives and lax.ppermute only.
A program may use at most 128 MiB of HBM per device.

v0:
```python
import math

import jax
import jax.numpy as jnp
from jax import lax
from jax.sharding import PartitionSpec as P

GW = 128
TILE = 512


def sent_together(arrays, axis, dim, along):
    widths = [math.prod(a.shape[along:]) for a in arrays]
    both = jnp.concatenate(
        [a.reshape(*a.shape[:along], w) for a, w in zip(arrays, widths)], axis=along
    )
    filled = lax.psum_scatter(both, axis, scatter_dimension=dim, tiled=True)
    tiles = jnp.split(filled, [sum(widths[:k]) for k in range(1, len(widths))], axis=along)
    return tuple(
        (b.reshape(*filled.shape[:along], *a.shape[along:]) for a, b in zip(arrays, tiles))
    )


def sent_together_2(arrays, axis, dim, along):
    widths = [math.prod(a.shape[along:]) for a in arrays]
    both = jnp.concatenate(
        [a.reshape(*a.shape[:along], w) for a, w in zip(arrays, widths)], axis=along
    )
    filled = lax.all_gather(both, axis, axis=dim, tiled=True)
    tiles = jnp.split(filled, [sum(widths[:k]) for k in range(1, len(widths))], axis=along)
    return tuple(
        (b.reshape(*filled.shape[:along], *a.shape[along:]) for a, b in zip(arrays, tiles))
    )


def group_vector(values, groups, group_count):
    choose = (groups[:, :, None] == jnp.arange(group_count, dtype=jnp.int32)[None, None, :]).astype(
        jnp.float32
    )
    return jnp.einsum("nrg,nrw->gw", choose, values, precision=lax.Precision.HIGHEST).reshape(-1)


def place_blocks(blocks, groups, slot_lookup, group_start, slot_count, per_tile, tile_side):
    chans_total, group_parts, run_width = (blocks.shape[0], blocks.shape[1], blocks.shape[2])
    sub_blocks = jnp.transpose(blocks, (0, 1, 3, 2, 4)).reshape(
        chans_total * group_parts * group_parts, run_width, run_width
    )
    row_group = jnp.broadcast_to(groups[:, :, None], (chans_total, group_parts, group_parts))
    col_group = jnp.broadcast_to(groups[:, None, :], (chans_total, group_parts, group_parts))
    tile_ids = row_group // per_tile * tile_side + col_group // per_tile
    slot_ids = slot_lookup[tile_ids] - group_start
    inside = jnp.logical_and(slot_ids >= 0, slot_ids < slot_count)
    slot_ids = jnp.where(inside, slot_ids, slot_count).reshape(-1)
    row_offset = (row_group % per_tile).reshape(-1)
    col_offset = (col_group % per_tile).reshape(-1)
    placed_buffer = jnp.zeros((slot_count, per_tile, per_tile, run_width, run_width), jnp.float32)
    placed_buffer = placed_buffer.at[slot_ids, row_offset, col_offset].add(sub_blocks, mode="drop")
    side_len = per_tile * run_width
    return jnp.transpose(placed_buffer, (0, 1, 3, 2, 4)).reshape(slot_count, side_len, side_len)


def local(effects, nominal, observed, mc_variance, theta, nuisance_index, bin_counts, tile_owner):
    chan_size = lax.axis_size("chan")
    bins_size = lax.axis_size("bins")
    chan_index = lax.axis_index("chan")
    bins_index = lax.axis_index("bins")
    chans_local, bins_local, width = effects.shape
    total_nu = theta.shape[0]
    group_parts = width // GW
    group_count = total_nu // GW
    per_tile = TILE // GW
    tile_side = total_nu // TILE
    chans_here = chans_local // bins_size
    tile_total = tile_owner.shape[0]
    tiles_dev = tile_total // (chan_size * bins_size)
    slice_len = total_nu // (chan_size * bins_size)
    groups_all = nuisance_index[:, ::GW] // GW
    local_groups = lax.dynamic_slice_in_dim(groups_all, chan_index * chans_local, chans_local, 0)
    chosen = (
        theta.reshape(group_count, GW)[local_groups]
        .reshape(chans_local, width)
        .astype(jnp.bfloat16)
    )
    exponent = jnp.einsum("cbk,ck->cb", effects, chosen, preferred_element_type=jnp.float32)
    expected = nominal * jnp.exp(exponent)
    denominator = 1.0 + expected * mc_variance
    positions = bins_index * bins_local + lax.broadcasted_iota(
        jnp.int32, (chans_local, bins_local), 1
    )
    live = positions < bin_counts[:, None]
    residual = jnp.where(live, (expected - observed) / denominator, 0.0)
    weight = jnp.where(live, expected / denominator, 0.0)
    scaled = (jnp.sqrt(weight)[:, :, None] * effects).astype(jnp.bfloat16)
    gradient_part = jnp.einsum(
        "cbk,cb->ck", effects, residual.astype(jnp.bfloat16), preferred_element_type=jnp.float32
    )
    blocks = jnp.einsum("cbk,cbl->ckl", scaled, scaled, preferred_element_type=jnp.float32)
    mine_blocks, mine_grads = sent_together((blocks, gradient_part), "bins", 0, 2)
    group_start = chan_index * bins_size * tiles_dev
    slot_lookup = (
        jnp.zeros((tile_total,), jnp.int32)
        .at[tile_owner]
        .set(jnp.arange(tile_total, dtype=jnp.int32))
    )
    gathered_order = jnp.arange(chan_size * chans_here, dtype=jnp.int32)
    channel_ids = (
        gathered_order // chans_here * chans_local
        + bins_index * chans_here
        + gathered_order % chans_here
    )
    gathered_groups = groups_all[channel_ids]
    every_blocks, every_grads = sent_together_2((mine_blocks, mine_grads), "chan", 0, 2)
    tiles_part = place_blocks(
        every_blocks.reshape(every_blocks.shape[0], group_parts, GW, group_parts, GW),
        gathered_groups,
        slot_lookup,
        group_start,
        bins_size * tiles_dev,
        per_tile,
        tile_side,
    )
    grad_vector = group_vector(
        every_grads.reshape(-1, group_parts, GW), gathered_groups, group_count
    )
    tile_sums, grad_rows = (
        lax.psum_scatter(tiles_part, "bins", scatter_dimension=0, tiled=True),
        lax.psum_scatter(
            grad_vector.reshape(chan_size, -1), "bins", scatter_dimension=1, tiled=True
        ),
    )
    grad_sum = lax.dynamic_slice_in_dim(grad_rows, chan_index, 1, 0).reshape(-1)
    slot_index = chan_index * bins_size + bins_index
    mine_ids = lax.dynamic_slice_in_dim(tile_owner, slot_index * tiles_dev, tiles_dev, 0)
    on_diagonal = (mine_ids // tile_side == mine_ids % tile_side).astype(jnp.float32)
    hessian_tiles = tile_sums + on_diagonal[:, None, None] * jnp.eye(TILE, dtype=jnp.float32)[None]
    gradient = grad_sum + lax.dynamic_slice_in_dim(theta, slot_index * slice_len, slice_len, 0)
    return (hessian_tiles, gradient)


def solution(mesh):
    return jax.shard_map(
        local,
        mesh=mesh,
        in_specs=(
            P("chan", "bins", None),
            P("chan", "bins"),
            P("chan", "bins"),
            P("chan", "bins"),
            P(),
            P(),
            P("chan"),
            P(),
        ),
        out_specs=(P(("chan", "bins"), None, None), P(("chan", "bins"))),
        check_vma=False,
    )
```

profile of v0, /device:TPU:1, one launch (start us, length us, event | category | flops | bytes accessed | tf_op | source)
XLA Modules:
  0.0 320.2 jit_solution(5230648610969269702)
XLA Ops:
  7.2 0.0 copy-start.5
  7.2 0.0 copy-start.1
  7.2 0.0 copy-start.3
  7.2 0.0 copy-start.2
  7.2 0.0 reduce-scatter.6.cloned.1.call-start
  7.3 1.1 slice.4
  8.4 0.1 add_select_fusion
  8.5 0.1 reshape.251
  8.6 1.3 gather_fusion.2
  9.9 0.0 copy-start
  9.9 5.8 %fusion.19 = f32[8,1,2048]{2,1,0:T(1,128)S(1)} fusion(bf16[8,256,1]{1,2,0:T(2,128)(2,1)S(1)} %reshape.286, bf16[8,2048,256]{2,1,0:T(8,128)(2,1)} %param.8), kind=kOutput, calls=%fused_computation.68 | convolution fusion | flops 8388608 | bytes 8458240 | tf_op jit(solution)/shard_map/cbk,ck->cb/dot_general | solution.py:84
  15.7 0.0 copy-done.5
  15.7 0.0 copy-done.1
  15.7 0.0 copy-done.3
  15.8 0.0 copy-done.2
  15.8 0.1 fusion.4
  15.9 0.0 copy-done
  15.9 1.2 fusion.7
  17.1 0.0 copy-start.4
  17.1 9.6 %fusion = f32[8,256,256]{1,2,0:T(8,128)S(1)} fusion(bf16[8,2048,256]{2,1,0:T(8,128)(2,1)S(1)} %copy-done, f32[8,2048]{1,0:T(8,128)S(1)} %get-tuple-element.2), kind=kOutput, calls=%fused_computation.6 | convolution fusion | flops 2160066560 | bytes 10551296 | tf_op jit(solution)/shard_map/cbk,cbl->ckl/dot_general | solution.py:97
  26.7 1.6 pad_maximum_fusion
  28.2 0.0 reduce-scatter.6.cloned.1.call-update
  28.2 0.0 all-gather.2.cloned.1.call-start
  28.3 38.0 %reduce-scatter.6.cloned.1.call-done = f32[1,256,257]{1,2,0:T(8,128)} async-done(((f32[8,256,257]{1,2,0:T(8,128)}), f32[1,256,257]{1,2,0:T(8,128)}) %reduce-scatter.6.cloned.1.call-update) | async-done | bytes 263184 | tf_op jit(solution)/shard_map/reduce_scatter | solution.py:17
  66.3 0.0 all-gather.2.cloned.1.call-update
  66.4 0.0 reduce-scatter.10.cloned.1.call-start
  66.4 0.6 gather_fusion
  67.0 0.1 copy.29
  67.1 0.2 compare_select_fusion
  67.3 0.1 reshape.243
  67.5 0.2 broadcast_select_fusion.1
  67.6 0.1 select_n.180
  67.8 0.1 select_n.183
  67.9 0.0 copy-done.4
  68.0 1.4 scatter_custom_fusion
  69.4 1.3 gather_fusion.1
  70.6 98.0 %all-gather.2.cloned.1.call-done = f32[32,256,257]{1,2,0:T(8,128)} async-done(((f32[1,256,257]{1,2,0:T(8,128)}), f32[32,256,257]{1,2,0:T(8,128)}) %all-gather.2.cloned.1.call-update) | async-done | bytes 8421392 | tf_op jit(solution)/shard_map/all_gather | solution.py:29
  168.7 1.0 split.11
  169.6 0.3 convolution_bitcast_fusion
  169.9 0.8 copy.38
  170.7 0.0 reduce-scatter.10.cloned.1.call-update
  170.7 0.2 reduce-scatter.8.cloned.1.call-start
  171.0 7.5 %split.10 = f32[32,256,256]{1,2,0:T(8,128)} slice(f32[32,256,257]{1,2,0:T(8,128)} %all-gather.2.cloned.1.call-done), slice={[0:32], [0:256], [0:256]} | slice | bytes 16777216 | tf_op jit(solution)/shard_map/split | solution.py:30
  178.4 10.8 %reshape.287 = f32[32,2,128,2,128]{2,1,4,3,0:T(2,128)} reshape(f32[32,256,256]{1,2,0:T(8,128)} %split.10) | data formatting | bytes 16777216 | tf_op jit(solution)/shard_map/reshape | solution.py:114
  189.3 13.2 %copy.27 = f32[32,2,2,128,128]{4,3,2,1,0:T(8,128)} copy(f32[32,2,2,128,128]{3,1,4,2,0:T(2,128)} %bitcast.44) | data formatting | bytes 16777216 | tf_op jit(solution)/shard_map/transpose | solution.py:45
  202.4 4.3 %broadcast_in_dim.59 = f32[8,4,4,128,128]{4,3,2,1,0:T(8,128)} broadcast(f32[]{:T(128)} %constant.128.clone.1), dimensions={} | broadcast | bytes 8388612 | tf_op jit(solution)/shard_map/broadcast_in_dim | solution.py:56
  206.7 28.3 %scatter_fusion = f32[8,4,4,128,128]{4,3,2,1,0:T(8,128)} fusion(f32[8,4,4,128,128]{4,3,2,1,0:T(8,128)} %broadcast_in_dim.59, s32[128]{0:T(128)S(1)} %fusion.18, f32[128,128,128]{2,1,0:T(8,128)} %bitcast.43), kind=kCustom, calls=%fused_computation.4 | custom fusion | flops 2097152 | bytes 25167360 | tf_op jit(solution)/shard_map/scatter-add | solution.py:57
  235.0 13.8 %copy.28 = f32[8,4,128,4,128]{4,3,2,1,0:T(4,128)} copy(f32[8,4,128,4,128]{4,2,3,1,0:T(8,128)} %bitcast.42) | data formatting | bytes 16777216 | tf_op jit(solution)/shard_map/transpose | solution.py:59
  248.8 10.3 %reshape.230 = f32[8,512,512]{2,1,0:T(8,128)} reshape(f32[8,4,128,4,128]{4,3,2,1,0:T(4,128)} %copy.28) | data formatting | bytes 16777216 | tf_op jit(solution)/shard_map/reshape | solution.py:59
  259.1 0.0 reduce-scatter.8.cloned.1.call-update
  259.1 0.6 dynamic_slice.13
  262.3 0.0 reduce-scatter.10.cloned.1.call-done
  262.4 0.8 constant_dynamic-slice_fusion
  263.2 0.1 copy.40
  263.2 1.3 bitcast_add_fusion
  264.5 46.9 %reduce-scatter.8.cloned.1.call-done = f32[1,512,512]{2,1,0:T(8,128)} async-done(((f32[8,512,512]{2,1,0:T(8,128)}), f32[1,512,512]{2,1,0:T(8,128)}) %reduce-scatter.8.cloned.1.call-update) | async-done | bytes 1048592 | tf_op jit(solution)/shard_map/reduce_scatter | solution.py:126
  311.4 2.3 select_add_fusion
  (15 shorter events, 0.1 us)
Async XLA Ops:
  7.2 8.6 %copy-start.5 = (s32[8]{0:T(128)S(1)}, s32[8]{0:T(128)}, u32[]{:S(2)}) copy-start(s32[8]{0:T(128)} %param.14) | copy-start | bytes 100
  7.2 8.6 %copy-start.1 = (f32[8,2048]{1,0:T(8,128)S(1)}, f32[8,2048]{1,0:T(8,128)}, u32[]{:S(2)}) copy-start(f32[8,2048]{1,0:T(8,128)} %param.11) | copy-start | bytes 196612
  7.2 8.6 %copy-start.3 = (s32[8,2048]{1,0:T(8,128)S(1)}, s32[8,2048]{1,0:T(8,128)}, u32[]{:S(2)}) copy-start(s32[8,2048]{1,0:T(8,128)} %param.10) | copy-start | bytes 196612
  7.2 8.6 %copy-start.2 = (f32[8,2048]{1,0:T(8,128)S(1)}, f32[8,2048]{1,0:T(8,128)}, u32[]{:S(2)}) copy-start(f32[8,2048]{1,0:T(8,128)} %param.9) | copy-start | bytes 196612
  7.2 59.1 %reduce-scatter.6.cloned.1.call-start = ((), (), s32[]{:S(2)}) async-start(), calls=%async_computation.3 | async-start | bytes 2433024 | tf_op jit(solution)/shard_map/reduce_scatter | solution.py:17
  9.9 5.9 %copy-start = (bf16[8,2048,256]{2,1,0:T(8,128)(2,1)S(1)}, bf16[8,2048,256]{2,1,0:T(8,128)(2,1)}, u32[]{:S(2)}) copy-start(bf16[8,2048,256]{2,1,0:T(8,128)(2,1)} %param.8) | copy-start | bytes 25165828
  17.1 50.8 %copy-start.4 = (s32[256]{0:T(256)S(1)}, s32[256]{0:T(256)}, u32[]{:S(2)}) copy-start(s32[256]{0:T(256)} %param.15) | copy-start | bytes 3076
  28.2 140.4 %all-gather.2.cloned.1.call-start = ((), (), s32[]{:S(2)}) async-start(), calls=%async_computation.4 | async-start | bytes 8921088 | tf_op jit(solution)/shard_map/all_gather | solution.py:29
  66.4 196.0 %reduce-scatter.10.cloned.1.call-start = ((), (), s32[]{:S(2)}) async-start(), calls=%async_computation.6 | async-start | bytes 147456
  170.7 140.7 %reduce-scatter.8.cloned.1.call-start = ((), (), s32[]{:S(2)}) async-start(), calls=%async_computation.5 | async-start | bytes 9437184 | tf_op jit(solution)/shard_map/reduce_scatter | solution.py:126
Sparse Core Ops, SparseCore 0:
  28.4 37.9 reduce-scatter.5
  68.9 99.6 all-gather.1
  171.7 28.9 reduce-scatter.9
  259.2 52.0 reduce-scatter.7
where the time goes:
time: 321 us; the launch traced here: 320 us
  waiting for transfers between devices  183 us (57%)
  local copies, waits for them, and re-layouts  69.3 us (22%)
  other arithmetic  34.1 us (11%)
  matrix products  16.8 us (5%)
  between operations  16.6 us (5%)
    all_gather x1, waiting for transfers between devices, sent_together_2(): filled = lax.all_gather(both, axis, axis=dim, tiled=True)  98 us
    reduce_scatter x1, waiting for transfers between devices, local(): lax.psum_scatter(tiles_part, 'bins', scatter_dimension=0, tiled=True)  46.9 us
    reduce_scatter x1, waiting for transfers between devices, sent_together(): filled = lax.psum_scatter(both, axis, scatter_dimension=dim, tiled=True)  38 us
    scatter-add x1, other arithmetic, place_blocks(): placed_buffer.at[slot_ids, row_offset, col_offset]  28.3 us
    transpose x1, local copies, waits for them, and re-layouts, place_blocks(): jnp.transpose(placed_buffer, (0, 1, 3, 2, 4))  13.8 us
    transpose x1, local copies, waits for them, and re-layouts, place_blocks(): jnp.transpose(blocks, (0, 1, 3, 2, 4))  13.2 us
    reshape x1, local copies, waits for them, and re-layouts, local(): every_blocks.reshape(every_blocks.shape[0], group_parts, GW, group_parts,...  10.8 us
    reshape x1, local copies, waits for them, and re-layouts, place_blocks(): jnp.transpose(placed_buffer, (0, 1, 3, 2, 4))  10.3 us
  transfers between devices with their start and end apart: 4, of which 3 were waited for; matrix products, arithmetic and copies ran while one was open for 30% of the time, Pallas kernels for 0%

commit v1 on v0

v1 whole, which is shorter than its diff:
```python
import jax
import jax.numpy as jnp
from jax import lax
from jax.experimental import pallas as pl
from jax.experimental.pallas import tpu as pltpu
from jax.sharding import PartitionSpec as P

GW = 128
TILE = 512
NY, NZ, NX, NC = 4, 8, 4, 2
QA, QB = 18, 17
GROUP_A, GROUP_B = 4, 8
F32, BF16 = jnp.float32, jnp.bfloat16


def z_shift(s):
    return [(y * NZ + z, y * NZ + (z + s) % NZ) for y in range(NY) for z in range(NZ)]


def y_shift(s):
    return [(y * NZ + z, (y + s) % NY * NZ + z) for y in range(NY) for z in range(NZ)]


def x_shift(s, flip):
    return [(x * NC + c, (x + s) % NX * NC + (c ^ flip)) for x in range(NX) for c in range(NC)]


def on_chan(value, perm):
    return lax.ppermute(value, "chan", perm)


def joined(parts):
    return parts[0] if len(parts) == 1 else jnp.concatenate(parts, axis=0)


def z_ring(pieces):
    count = len(pieces)
    found = {0: list(pieces)}
    up, down = list(pieces), list(pieces)
    for s in (1, 2, 3):
        up = [on_chan(v, z_shift(1)) for v in up]
        down = [on_chan(v, z_shift(-1)) for v in down]
        found[s], found[NZ - s] = up, down
    half = (count + 1) // 2
    found[4] = [
        on_chan(up[k], z_shift(1)) if k < half else on_chan(down[k], z_shift(-1)) for k in range(count)
    ]
    return found


def y_ring(pieces):
    count = len(pieces)
    up = [on_chan(v, y_shift(1)) for v in pieces]
    down = [on_chan(v, y_shift(-1)) for v in pieces]
    half = (count + 1) // 2
    far = [
        on_chan(up[k], y_shift(1)) if k < half else on_chan(down[k], y_shift(-1)) for k in range(count)
    ]
    return {0: list(pieces), 1: up, 2: far, 3: down}


def gather_a(own):
    first = [own] + [on_chan(own, y_shift(d)) for d in (1, 2, 3)]
    pieces = [joined(first[k : k + GROUP_A]) for k in range(0, NY, GROUP_A)]
    found = z_ring(pieces)
    where = {
        (dy, dz): (found[dz][dy // GROUP_A], dy % GROUP_A * QA) for dy in range(NY) for dz in range(NZ)
    }
    return where


def gather_b(own):
    around = z_ring([own])
    first = [around[d][0] for d in range(NZ)]
    pieces = [joined(first[k : k + GROUP_B]) for k in range(0, NZ, GROUP_B)]
    found = y_ring(pieces)
    where = {
        (dy, dz): (found[dy][dz // GROUP_B], dz % GROUP_B * QB) for dy in range(NY) for dz in range(NZ)
    }
    return where


def pack_kernel(place_ref, blocks_ref, grad_ref, mine_ref, other_ref, a_ref, o_ref, b_ref):
    x, core = place_ref[0], place_ref[1]
    for c in range(8):
        rows = slice(c * GW, (c + 1) * GW)
        a_ref[rows] = blocks_ref[c * 256 : c * 256 + GW, :GW]
        o_ref[rows] = blocks_ref[c * 256 : c * 256 + GW, GW:]
        b_ref[rows] = blocks_ref[c * 256 + GW : c * 256 + 256, GW:]
    lane = lax.broadcasted_iota(jnp.int32, (8, GW), 1)
    diag = jnp.zeros((8, GW), F32)
    for row in range(GW):
        a = a_ref[pl.ds(row, 8, stride=GW), :]
        diag = jnp.where(lane == row, a, diag)
    grads = grad_ref[...]
    for d in range(NX):
        for ref, side in ((mine_ref, core), (other_ref, 1 - core)):
            start = lax.rem(x + d, NX) * 32 + side * 16
            for q in range(16):
                row = start + q
                ref[d, q] = o_ref[pl.ds(row, 8, stride=GW), :]
                a = a_ref[pl.ds(row, 8, stride=GW), :]
                b = b_ref[pl.ds(row, 8, stride=GW), :]
                ref[d, QA + q] = jnp.where(lane > row, a, b)
            ref[d, 16] = grads[:, :GW]
            ref[d, 17] = grads[:, GW:]
            ref[d, QA + 16] = diag


def split2(v):
    high = v.astype(BF16)
    return high, (v - high.astype(F32)).astype(BF16)


def place_kernel(arrays, offsets_a, offsets_b, place_ref, meta_ref, *refs):
    ins, (mine_ref, other_ref, grad_ref) = refs[:arrays], refs[arrays:]
    core, slice_index, x = place_ref[1], place_ref[2], place_ref[0]
    pos = lax.broadcasted_iota(jnp.int32, (128, 256), 0)
    meta = meta_ref[...]

    def hot(*rows):
        hit = pos == meta[rows[0] : rows[0] + 1]
        for r in rows[1:]:
            hit = jnp.logical_or(hit, pos == meta[r : r + 1])
        return jnp.where(hit, 1.0, 0.0).astype(BF16)

    sel_off = hot(0, 1)
    sel_both = jnp.concatenate([hot(2), hot(3)], axis=0)
    lane = lax.broadcasted_iota(jnp.int32, (128, GW), 1)

    def gathered(offsets, q):
        return jnp.concatenate([ins[k][o + q] for k, o in offsets], axis=0)

    def apply(sel, v):
        high, low = split2(v)
        return jnp.dot(sel, high, preferred_element_type=F32) + jnp.dot(
            sel, low, preferred_element_type=F32
        )

    diag = apply(sel_both[:128], gathered(offsets_b, 16))
    grads = apply(hot(4)[:8], gathered(offsets_a, 16)) + apply(hot(5)[:8], gathered(offsets_a, 17))
    grad_ref[...] = grads
    for q in range(0, 16, 2):
        off = apply(
            sel_off, jnp.concatenate([gathered(offsets_a, q), gathered(offsets_a, q + 1)], axis=1)
        )
        both = apply(
            sel_both, jnp.concatenate([gathered(offsets_b, q), gathered(offsets_b, q + 1)], axis=1)
        )
        for k in range(2):
            row = slice_index * 16 + q + k
            cols = slice(k * GW, (k + 1) * GW)
            upper, lower = both[:128, cols], both[128:, cols]
            value = off[:, cols] + jnp.where(lane > row, upper, lower)
            value = value + jnp.where(lane == row, diag, 0.0)
            value = value.reshape(NX, NC, 16, GW)
            del upper, lower
            for d in range(NX):
                mine_ref[d, q + k] = value[d, 0]
                other_ref[d, q + k] = value[d, 1]


def finish_kernel(place_ref, *refs):
    ins, out_ref, tile_ref = refs[:8], refs[8], refs[9]
    x, core, tile_row, tile_col = place_ref[0], place_ref[1], place_ref[3], place_ref[4]
    k = 0
    for flip in range(NC):
        for d in range(NX):
            source = lax.rem(x - d + NX, NX) * 2 + (core + flip) % 2
            for rc in range(16):
                start = pl.multiple_of(source * 16 + rc // 4 * GW, 16)
                tile_ref[pl.ds(start, 16), rc % 4 * GW : (rc % 4 + 1) * GW] = ins[k][
                    pl.ds(rc, 16, stride=16), :
                ]
            k += 1

    @pl.when(tile_row < tile_col)
    def _():
        out_ref[0] = tile_ref[...]

    @pl.when(tile_row > tile_col)
    def _():
        for r in range(4):
            for c in range(4):
                out_ref[0, r * GW : (r + 1) * GW, c * GW : (c + 1) * GW] = tile_ref[
                    c * GW : (c + 1) * GW, r * GW : (r + 1) * GW
                ].T

    @pl.when(tile_row == tile_col)
    def _():
        row = lax.broadcasted_iota(jnp.int32, (GW, GW), 0)
        col = lax.broadcasted_iota(jnp.int32, (GW, GW), 1)
        for r in range(4):
            for c in range(4):
                here = tile_ref[r * GW : (r + 1) * GW, c * GW : (c + 1) * GW]
                there = tile_ref[c * GW : (c + 1) * GW, r * GW : (r + 1) * GW].T
                value = here + there
                if r == c:
                    value = jnp.where(row == col, here + 1.0, value)
                out_ref[0, r * GW : (r + 1) * GW, c * GW : (c + 1) * GW] = value


VMEM = pl.BlockSpec(memory_space=pltpu.VMEM)
SMEM = pl.BlockSpec(memory_space=pltpu.SMEM)


def shape(*dims):
    return jax.ShapeDtypeStruct(dims, F32)


def cost(flops, moved):
    return pl.CostEstimate(flops=flops, bytes_accessed=moved, transcendentals=0)


def local(effects, nominal, observed, mc_variance, theta, nuisance_index, bin_counts, tile_owner):
    chan_index, bins_index = lax.axis_index("chan"), lax.axis_index("bins")
    y, z, x, core = chan_index // NZ, chan_index % NZ, bins_index // NC, bins_index % NC
    chans, bins, width = effects.shape
    tile_side = theta.shape[0] // TILE
    groups = nuisance_index[:, ::GW] // GW
    own_groups = lax.dynamic_slice_in_dim(groups, chan_index * chans, chans, 0)
    chosen = theta.reshape(-1, GW)[own_groups].reshape(chans, width).astype(BF16)
    slot = chan_index * (NX * NC) + bins_index
    own_tile = lax.dynamic_slice_in_dim(tile_owner, slot, 1, 0)[0]
    place = jnp.stack([x, core, bins_index, own_tile // tile_side, own_tile % tile_side]).astype(jnp.int32)

    exponent = jnp.einsum("cbk,ck->cb", effects, chosen, preferred_element_type=F32)
    expected = nominal * jnp.exp(exponent)
    denominator = 1.0 + expected * mc_variance
    positions = bins_index * bins + lax.broadcasted_iota(jnp.int32, (chans, bins), 1)
    live = positions < bin_counts[:, None]
    residual = jnp.where(live, (expected - observed) / denominator, 0.0)
    weight = jnp.where(live, expected / denominator, 0.0)
    scaled = (jnp.sqrt(weight)[:, :, None] * effects).astype(BF16)
    grads = jnp.einsum("cbk,cb->ck", effects, residual.astype(BF16), preferred_element_type=F32)
    blocks = jnp.einsum("cbk,cbl->ckl", scaled, scaled, preferred_element_type=F32)

    tiles = QA + QB
    mine, other = pl.pallas_call(
        pack_kernel,
        out_shape=[shape(NX, tiles, 8, GW)] * 2,
        in_specs=[SMEM, VMEM, VMEM],
        out_specs=[VMEM] * 2,
        scratch_shapes=[pltpu.VMEM((8 * GW, GW), F32)] * 3,
        cost_estimate=cost(10**6, 4 * 10**6),
        name="pack",
    )(place, blocks.reshape(chans * width, width), grads)
    other = lax.ppermute(other, "bins", x_shift(0, 1))
    chip = [mine[d] + other[d] for d in range(NX)]
    arrived = [lax.ppermute(chip[d], "bins", x_shift(d, 0)) for d in (1, 2, 3)]
    own_a = chip[0][:QA] + arrived[0][:QA] + arrived[1][:QA] + arrived[2][:QA]
    own_b = chip[0][QA:] + arrived[0][QA:] + arrived[1][QA:] + arrived[2][QA:]

    at_a, at_b = gather_a(own_a), gather_b(own_b)
    order = [(dy, dz) for dy in range(NY) for dz in range(NZ)]
    arrays, offsets_a, offsets_b = [], [], []
    for at, offsets in ((at_a, offsets_a), (at_b, offsets_b)):
        for key in order:
            array, offset = at[key]
            known = [k for k, v in enumerate(arrays) if v is array]
            if not known:
                arrays.append(array)
                known = [len(arrays) - 1]
            offsets.append((known[0], offset))

    dy = jnp.arange(NY, dtype=jnp.int32)[:, None, None]
    dz = jnp.arange(NZ, dtype=jnp.int32)[None, :, None]
    channel = ((y - dy + NY) % NY * NZ + (z - dz + NZ) % NZ) * chans
    channel = (channel + jnp.arange(chans, dtype=jnp.int32)).reshape(-1)
    first, second = groups[channel, 0], groups[channel, 1]
    rel_x = jnp.arange(NX, dtype=jnp.int32)
    row_tiles = lax.dynamic_slice_in_dim(tile_owner, chan_index * 8, 8, 0)
    rel = (jnp.arange(8, dtype=jnp.int32) // NC - x + NX) % NX * NC + (jnp.arange(8, dtype=jnp.int32) + core) % NC
    per = TILE // GW

    def slot_of(tile_ids, inside):
        hit = row_tiles[:, None] == tile_ids[None, :]
        base = jnp.sum(jnp.where(hit, rel[:, None] * 16 + inside[None, :] + 1, 0), axis=0)
        return base - 1

    tr, tc = first // per, second // per
    inside = first % per * per + second % per
    straight = slot_of(tr * tile_side + tc, inside)
    mirrored = jnp.where(tr == tc, -1, slot_of(tc * tile_side + tr, inside))
    upper = slot_of(tr * (tile_side + 1), first % per * (per + 1))
    lower = slot_of(tc * (tile_side + 1), second % per * (per + 1))
    meta = jnp.stack(
        [straight, mirrored, upper, lower, first - 2 * chan_index, second - 2 * chan_index, upper, lower]
    )
    del rel_x

    import functools

    mine, other, grad_rows = pl.pallas_call(
        functools.partial(place_kernel, len(arrays), offsets_a, offsets_b),
        out_shape=[shape(NX, 16, 16, GW)] * 2 + [shape(8, GW)],
        in_specs=[SMEM, VMEM] + [VMEM] * len(arrays),
        out_specs=[VMEM] * 3,
        cost_estimate=cost(10**9, 6 * 10**6),
        name="place",
    )(place, meta, *arrays)

    ins = [mine[0]] + [lax.ppermute(mine[d], "bins", x_shift(d, 0)) for d in (1, 2, 3)]
    ins += [lax.ppermute(other[d], "bins", x_shift(d, 1)) for d in range(NX)]
    hessian_tiles = pl.pallas_call(
        finish_kernel,
        out_shape=shape(1, TILE, TILE),
        in_specs=[SMEM] + [VMEM] * 8,
        out_specs=VMEM,
        scratch_shapes=[pltpu.VMEM((TILE, TILE), F32)],
        cost_estimate=cost(10**6, 2 * 10**6),
        name="finish",
    )(place, *[v.reshape(256, GW) for v in ins])

    part = lax.dynamic_slice(
        grad_rows, (bins_index // 4, bins_index % 4 * 32), (1, 32)
    ).reshape(-1)
    gradient = part + lax.dynamic_slice_in_dim(theta, slot * 32, 32, 0)
    return hessian_tiles, gradient


def solution(mesh):
    return jax.shard_map(
        local,
        mesh=mesh,
        in_specs=(
            P("chan", "bins", None),
            P("chan", "bins"),
            P("chan", "bins"),
            P("chan", "bins"),
            P(),
            P(),
            P("chan"),
            P(),
        ),
        out_specs=(P(("chan", "bins"), None, None), P(("chan", "bins"))),
        check_vma=False,
    )
```

time: 321 us -> 139 us (0.43)
  waiting for transfers between devices: 183 us -> 44.8 us
  local copies, waits for them, and re-layouts: 69.3 us -> 14.2 us
  starting transfers between devices: 0.34 us -> 44.2 us
  other arithmetic: 34.1 us -> 3.13 us
  between operations: 16.6 us -> 3.7 us
  Pallas kernels: 0 us -> 11.2 us
    all_gather x1 -> x0, waiting for transfers between devices: 98 us -> none  [sent_together_2(): filled = lax.all_gather(both, axis, axis=dim, tiled=True)]
    reduce_scatter x2 -> x0, waiting for transfers between devices: 84.9 us -> none  [the longest x1 46.9 us: local(): lax.psum_scatter(tiles_part, 'bins', scatter_dimension=0, tiled=True)]
    ppermute x0 -> x31, waiting for transfers between devices: none -> 44.8 us  [the longest x20 29.8 us: on_chan(): return lax.ppermute(value, 'chan', perm)]
    ppermute x0 -> x31, starting transfers between devices: none -> 44.2 us  [the longest x20 24.5 us: on_chan(): return lax.ppermute(value, 'chan', perm)]
    scatter-add x1 -> x0, other arithmetic: 28.3 us -> none  [place_blocks(): placed_buffer.at[slot_ids, row_offset, col_offset]]
    transpose x2 -> x0, local copies, waits for them, and re-layouts: 26.9 us -> none  [the longest x1 13.8 us: place_blocks(): jnp.transpose(placed_buffer, (0, 1, 3, 2, 4))]
    reshape x3 -> x0, local copies, waits for them, and re-layouts: 21.1 us -> none  [the longest x1 10.8 us: local(): every_blocks.reshape(every_blocks.shape[0], group_parts, GW, group_parts,...]
    pallas_call x0 -> x3, Pallas kernels: none -> 11.2 us  [the longest x1 4.42 us: local(): pl.pallas_call(functools.partial(place_kernel, len(arrays), offsets_a, of...]
  transfers between devices with their start and end apart: 4 -> 31, of which waited for: 3 -> 15; matrix products, arithmetic and copies ran while one was open for 30% -> 5% of each run, Pallas kernels for 0% -> 0%
where the time goes in v1:
time: 139 us; the launch traced here: 138 us
  waiting for transfers between devices  44.8 us (32%)
  starting transfers between devices  44.2 us (32%)
  matrix products  17.2 us (12%)
  local copies, waits for them, and re-layouts  14.2 us (10%)
  Pallas kernels  11.2 us (8%)
  between operations  3.7 us (3%)
  other arithmetic  3.13 us (2%)
    ppermute x20, waiting for transfers between devices, on_chan(): return lax.ppermute(value, 'chan', perm)  29.8 us
    ppermute x20, starting transfers between devices, on_chan(): return lax.ppermute(value, 'chan', perm)  24.5 us
    ppermute x4, starting transfers between devices, local(): ins += [lax.ppermute(other[d], 'bins', x_shift(d, 1)) for d in range(NX)]  13.1 us
    dot_general x1, matrix products, local(): jnp.einsum('cbk,cbl->ckl', scaled, scaled, preferred_element_type=F32)  10.2 us
    ppermute x3, waiting for transfers between devices, local(): arrived = [lax.ppermute(chip[d], 'bins', x_shift(d, 0)) for d in (1, 2, 3)]  9.03 us
    ppermute x4, waiting for transfers between devices, local(): ins += [lax.ppermute(other[d], 'bins', x_shift(d, 1)) for d in range(NX)]  5.93 us
    dot_general x1, matrix products, local(): jnp.einsum('cbk,ck->cb', effects, chosen, preferred_element_type=F32)  5.78 us
    pallas_call x1, Pallas kernels, local(): pl.pallas_call(functools.partial(place_kernel, len(arrays), offsets_a, of...  4.42 us
  transfers between devices with their start and end apart: 31, of which 15 were waited for; matrix products, arithmetic and copies ran while one was open for 5% of the time, Pallas kernels for 0%

profile of v1, /device:TPU:1, one launch (start us, length us, event | category | flops | bytes accessed | tf_op | source)
XLA Modules:
  0.0 138.4 jit_solution(4432611675755399484)
XLA Ops:
  0.7 1.3 dynamic_slice.15
  4.6 1.1 slice.81
  5.8 0.1 add_select_fusion
  5.9 0.1 reshape.434
  6.0 1.3 gather_fusion.2
  7.3 5.8 %fusion.26 = f32[8,1,2048]{2,1,0:T(1,128)S(1)} fusion(bf16[8,256,1]{1,2,0:T(2,128)(2,1)S(1)} %reshape.449, bf16[8,2048,256]{2,1,0:T(8,128)(2,1)} %param.8), kind=kOutput, calls=%fused_computation.132 | convolution fusion | flops 8388608 | bytes 8458240 | tf_op jit(solution)/shard_map/cbk,ck->cb/dot_general | solution.py:227
  13.1 0.1 fusion.12
  13.2 1.2 fusion.10
  14.4 0.6 copy.26
  15.0 10.2 %fusion = f32[8,256,256]{2,1,0:T(8,128)} fusion(bf16[8,2048,256]{2,1,0:T(8,128)(2,1)S(1)} %copy-done, f32[8,2048]{1,0:T(8,128)S(1)} %get-tuple-element.41), kind=kOutput, calls=%fused_computation.4 | convolution fusion | flops 2160066560 | bytes 10551296 | tf_op jit(solution)/shard_map/cbk,cbl->ckl/dot_general | solution.py:236
  25.3 0.6 stack.34.place_ref
  25.9 3.9 %pack.1 = (f32[4,35,8,128]{3,2,1,0:T(8,128)}, f32[4,35,8,128]{3,2,1,0:T(8,128)}) custom-call(s32[5]{0:T(128)} %stack.34.place_ref, f32[2048,256]{1,0:T(8,128)} %bitcast.73, f32[8,256]{1,0:T(8,128)} %bitcast.83), custom_call_target="tpu_custom_call" | custom-call | flops 1000000 | bytes 4000000 | tf_op jit(solution)/shard_map/pack/pallas_call | solution.py:239
  29.8 3.2 %collective-permute-start = (f32[4,35,8,128]{3,2,1,0:T(8,128)}, f32[4,35,8,128]{3,2,1,0:T(8,128)S(1)}, u32[]{:S(2)}, u32[]{:S(2)}) collective-permute-start(f32[4,35,8,128]{3,2,1,0:T(8,128)} %get-tuple-element.8), channel_id=1, source_target_pairs={{0,1},{1,0},{2,3},{3,2},{4,5},{5,4},{6,7},{7,6},{8,9},{9,8},{10,11... | collective-permute-start | bytes 1720328 | tf_op jit(solution)/shard_map/ppermute | solution.py:248
  33.1 0.1 iota_add_fusion
  33.1 0.1 add.425
  33.2 1.9 %gather_fusion.1 = s32[256]{0:T(256)S(1)} fusion(s32[256,2]{1,0:T(8,128)S(1)} %add_select_fusion, s32[256]{0:T(256)S(1)} %bitcast.72), kind=kCustom, calls=%fused_computation.1 | custom fusion | bytes 4096 | tf_op jit(solution)/shard_map/gather | solution.py:270
  35.2 1.9 %gather_fusion = s32[256]{0:T(256)S(1)} fusion(s32[256,2]{1,0:T(8,128)S(1)} %add_select_fusion, s32[256]{0:T(256)S(1)} %bitcast.71), kind=kCustom, calls=%fused_computation | custom fusion | bytes 4096 | tf_op jit(solution)/shard_map/gather | solution.py:270
  37.2 1.2 slice_add_fusion.3
  38.4 0.8 collective-permute-start.3
  39.3 0.5 collective-permute-start.2
  39.8 0.6 collective-permute-start.1
  40.4 0.1 dynamic_slice.16
  40.5 3.3 %collective-permute-done.3 = f32[35,8,128]{2,1,0:T(8,128)S(1)} collective-permute-done((f32[35,8,128]{2,1,0:T(8,128)S(1)}, f32[35,8,128]{2,1,0:T(8,128)S(1)}, u32[]{:S(2)}, u32[]{:S(2)}) %collective-permute-start.3) | collective-permute-done | bytes 143392 | tf_op jit(solution)/shard_map/ppermute | solution.py:250
  43.8 2.0 %collective-permute-done.2 = f32[35,8,128]{2,1,0:T(8,128)S(1)} collective-permute-done((f32[35,8,128]{2,1,0:T(8,128)S(1)}, f32[35,8,128]{2,1,0:T(8,128)S(1)}, u32[]{:S(2)}, u32[]{:S(2)}) %collective-permute-start.2) | collective-permute-done | bytes 143392 | tf_op jit(solution)/shard_map/ppermute | solution.py:250
  45.9 3.7 %collective-permute-done.1 = f32[35,8,128]{2,1,0:T(8,128)S(1)} collective-permute-done((f32[35,8,128]{2,1,0:T(8,128)S(1)}, f32[35,8,128]{2,1,0:T(8,128)S(1)}, u32[]{:S(2)}, u32[]{:S(2)}) %collective-permute-start.1) | collective-permute-done | bytes 143392 | tf_op jit(solution)/shard_map/ppermute | solution.py:250
  49.6 5.7 %collective-permute-start.18 = (f32[17,8,128]{2,1,0:T(8,128)S(1)}, f32[17,8,128]{2,1,0:T(8,128)S(1)}, u32[]{:S(2)}, u32[]{:S(2)}) collective-permute-start(f32[17,8,128]{2,1,0:T(8,128)S(1)} %get-tuple-element.19), channel_id=1, source_target_pairs={{0,56},{8,0},{16,8},{24,16},{32,24},{40,32},{48,40},{56,48},{64,12... | collective-permute-start | bytes 208904 | tf_op jit(solution)/shard_map/ppermute | solution.py:29
  55.2 2.8 %collective-permute-start.6 = (f32[18,8,128]{2,1,0:T(8,128)S(1)}, f32[18,8,128]{2,1,0:T(8,128)S(1)}, u32[]{:S(2)}, u32[]{:S(2)}) collective-permute-start(f32[18,8,128]{2,1,0:T(8,128)S(1)} %slice_add_fusion.4), channel_id=1, source_target_pairs={{0,192},{8,200},{16,208},{24,216},{32,224},{40,232},{48,240},{56,2... | collective-permute-start | bytes 221192 | tf_op jit(solution)/shard_map/ppermute | solution.py:29
  58.0 0.4 collective-permute-start.5
  58.4 0.7 collective-permute-start.4
  59.1 2.7 %collective-permute-start.19 = (f32[17,8,128]{2,1,0:T(8,128)S(1)}, f32[17,8,128]{2,1,0:T(8,128)S(1)}, u32[]{:S(2)}, u32[]{:S(2)}) collective-permute-start(f32[17,8,128]{2,1,0:T(8,128)S(1)} %collective-permute-done.18), channel_id=1, source_target_pairs={{0,56},{8,0},{16,8},{24,16},{32,24},{40,32},{48,40},{56,48},{64,12... | collective-permute-start | bytes 208904 | tf_op jit(solution)/shard_map/ppermute | solution.py:29
  61.8 1.0 collective-permute-done.5
  62.8 1.1 collective-permute-done.4
  63.9 2.4 %collective-permute-start.11 = (f32[72,8,128]{2,1,0:T(8,128)S(1)}, f32[72,8,128]{2,1,0:T(8,128)S(1)}, u32[]{:S(2)}, u32[]{:S(2)}) collective-permute-start(f32[72,8,128]{2,1,0:T(8,128)S(1)} %pad_maximum_fusion.refs_0_), channel_id=1, source_target_pairs={{0,56},{8,0},{16,8},{24,16},{32,24},{40,32},{48,40},{56,48},{64,12... | collective-permute-start | bytes 884744 | tf_op jit(solution)/shard_map/ppermute | solution.py:29
  66.3 2.7 %collective-permute-start.20 = (f32[17,8,128]{2,1,0:T(8,128)S(1)}, f32[17,8,128]{2,1,0:T(8,128)S(1)}, u32[]{:S(2)}, u32[]{:S(2)}) collective-permute-start(f32[17,8,128]{2,1,0:T(8,128)S(1)} %collective-permute-done.19), channel_id=1, source_target_pairs={{0,56},{8,0},{16,8},{24,16},{32,24},{40,32},{48,40},{56,48},{64,12... | collective-permute-start | bytes 208904 | tf_op jit(solution)/shard_map/ppermute | solution.py:29
  69.0 5.8 %collective-permute-done.16 = f32[17,8,128]{2,1,0:T(8,128)S(1)} collective-permute-done((f32[17,8,128]{2,1,0:T(8,128)S(1)}, f32[17,8,128]{2,1,0:T(8,128)S(1)}, u32[]{:S(2)}, u32[]{:S(2)}) %collective-permute-start.16) | collective-permute-done | bytes 69664 | tf_op jit(solution)/shard_map/ppermute | solution.py:29
  74.8 4.4 %collective-permute-done.17 = f32[17,8,128]{2,1,0:T(8,128)S(1)} collective-permute-done((f32[17,8,128]{2,1,0:T(8,128)S(1)}, f32[17,8,128]{2,1,0:T(8,128)S(1)}, u32[]{:S(2)}, u32[]{:S(2)}) %collective-permute-start.17) | collective-permute-done | bytes 69664 | tf_op jit(solution)/shard_map/ppermute | solution.py:29
  79.3 1.1 collective-permute-start.21
  80.4 0.1 select_reduce_fusion
  80.5 2.7 %collective-permute-start.12 = (f32[72,8,128]{2,1,0:T(8,128)S(1)}, f32[72,8,128]{2,1,0:T(8,128)}, u32[]{:S(2)}, u32[]{:S(2)}) collective-permute-start(f32[72,8,128]{2,1,0:T(8,128)S(1)} %collective-permute-done.11.refs_7_), channel_id=1, source_target_pairs={{0,56},{8,0},{16,8},{24,16},{32,24},{40,32},{48,40},{56,48},{64,12... | collective-permute-start | bytes 884744 | tf_op jit(solution)/shard_map/ppermute | solution.py:29
  83.2 3.9 %collective-permute-done.8.refs_2_ = f32[72,8,128]{2,1,0:T(8,128)S(1)} collective-permute-done((f32[72,8,128]{2,1,0:T(8,128)S(1)}, f32[72,8,128]{2,1,0:T(8,128)S(1)}, u32[]{:S(2)}, u32[]{:S(2)}) %collective-permute-start.8) | collective-permute-done | bytes 294944 | tf_op jit(solution)/shard_map/ppermute | solution.py:29
  87.2 1.7 %collective-permute-start.23 = (f32[136,8,128]{2,1,0:T(8,128)S(1)}, f32[136,8,128]{2,1,0:T(8,128)S(1)}, u32[]{:S(2)}, u32[]{:S(2)}) collective-permute-start(f32[136,8,128]{2,1,0:T(8,128)S(1)} %constant_dynamic-update-slice_fusion.refs_8_), channel_id=1, source_target_pairs={{0,192},{8,200},{16,208},{24,216},{32,224},{40,232},{48,240},{56,2... | collective-permute-start | bytes 1671176 | tf_op jit(solution)/shard_map/ppermute | solution.py:29
  88.9 1.1 collective-permute-done.21.refs_9_
  90.0 0.5 collective-permute-start.22
  90.5 1.1 collective-permute-start.13
  91.6 3.9 %collective-permute-done.9.refs_3_ = f32[72,8,128]{2,1,0:T(8,128)} collective-permute-done((f32[72,8,128]{2,1,0:T(8,128)S(1)}, f32[72,8,128]{2,1,0:T(8,128)}, u32[]{:S(2)}, u32[]{:S(2)}) %collective-permute-start.9) | collective-permute-done | bytes 294944 | tf_op jit(solution)/shard_map/ppermute | solution.py:29
  95.6 0.6 stack.35.meta_ref
  96.2 0.3 collective-permute-done.13.refs_5_
  96.5 8.3 %collective-permute-done.10.refs_4_ = f32[72,8,128]{2,1,0:T(8,128)} collective-permute-done((f32[72,8,128]{2,1,0:T(8,128)}, f32[72,8,128]{2,1,0:T(8,128)}, u32[]{:S(2)}, u32[]{:S(2)}) %collective-permute-start.10) | collective-permute-done | bytes 294944 | tf_op jit(solution)/shard_map/ppermute | solution.py:29
  104.8 0.8 copy-done.5
  105.6 4.4 %place.1 = (f32[4,16,16,128]{3,2,1,0:T(8,128)}, f32[4,16,16,128]{3,2,1,0:T(8,128)}, f32[8,128]{1,0:T(8,128)}) custom-call(s32[5]{0:T(128)} %stack.34.place_ref, s32[8,256]{1,0:T(8,128)} %stack.35.meta_ref, f32[72,8,128]{2,1,0:T(8,128)} %copy-done.1, f32[72,8,128]{2,1,0:T(8,128)} %copy-done.7, f32[72,8,128]{2,1,0:T(8,128)} %copy-done.8, ...), custom_call_target="tpu_custom_call" | custom-call | flops 1000000000 | bytes 6000000 | tf_op jit(solution)/shard_map/place/pallas_call | solution.py:294
  110.1 1.8 %slice_bitcast_fusion.4 = (f32[16,16,128]{2,1,0:T(8,128)S(1)}, f32[16,16,128]{2,1,0:T(8,128)S(1)}, f32[16,16,128]{2,1,0:T(8,128)S(1)}, f32[1,16,16,128]{3,2,1,0:T(8,128)}) fusion(f32[4,16,16,128]{3,2,1,0:T(8,128)} %get-tuple-element.9), kind=kLoop, calls=%fused_computation.23 | loop fusion | bytes 1048576 | tf_op jit(solution)/shard_map/squeeze | solution.py:303
  111.8 0.5 collective-permute-start.26
  112.3 0.5 collective-permute-start.25
  112.8 0.5 collective-permute-start.24
  113.3 1.1 slice_bitcast_fusion
  114.4 11.0 %collective-permute-start.30 = (f32[16,16,128]{2,1,0:T(8,128)S(1)}, f32[16,16,128]{2,1,0:T(8,128)S(1)}, u32[]{:S(2)}, u32[]{:S(2)}) collective-permute-start(f32[16,16,128]{2,1,0:T(8,128)S(1)} %get-tuple-element.32), channel_id=1, source_target_pairs={{0,7},{1,6},{2,1},{3,0},{4,3},{5,2},{6,5},{7,4},{8,15},{9,14},{10,... | collective-permute-start | bytes 393224 | tf_op jit(solution)/shard_map/ppermute | solution.py:304
  125.4 1.0 collective-permute-start.29
  126.5 1.0 collective-permute-start.28
  127.5 1.3 bitcast_add_fusion
  128.8 0.2 collective-permute-done.30
  129.0 3.1 %collective-permute-done.29 = f32[16,16,128]{2,1,0:T(8,128)S(1)} collective-permute-done((f32[16,16,128]{2,1,0:T(8,128)S(1)}, f32[16,16,128]{2,1,0:T(8,128)S(1)}, u32[]{:S(2)}, u32[]{:S(2)}) %collective-permute-start.29) | collective-permute-done | bytes 131104 | tf_op jit(solution)/shard_map/ppermute | solution.py:304
  132.1 2.6 %collective-permute-done.28 = f32[16,16,128]{2,1,0:T(8,128)S(1)} collective-permute-done((f32[16,16,128]{2,1,0:T(8,128)S(1)}, f32[16,16,128]{2,1,0:T(8,128)S(1)}, u32[]{:S(2)}, u32[]{:S(2)}) %collective-permute-start.28) | collective-permute-done | bytes 131104 | tf_op jit(solution)/shard_map/ppermute | solution.py:304
  134.8 0.6 copy-done.14
  135.5 2.9 %finish.1 = f32[1,512,512]{2,1,0:T(8,128)} custom-call(s32[5]{0:T(128)} %stack.34.place_ref, f32[256,128]{1,0:T(8,128)} %bitcast.74, f32[256,128]{1,0:T(8,128)} %bitcast.77, f32[256,128]{1,0:T(8,128)} %bitcast.76, f32[256,128]{1,0:T(8,128)} %bitcast.75, f32[256,128]{1,0:T(8,128)} %bitcast.81, f32[256,128]{1,0:T(8,128)} %bitcast.80, f32[256,128]{1,0:T(8,128)} %bitcast.79, ...), custom_call_target="tpu_custom_call" | custom-call | flops 1000000 | bytes 2000000 | tf_op jit(solution)/shard_map/finish/pallas_call | solution.py:305
  (92 shorter events, 0.6 us)
Async XLA Ops:
  0.6 12.5 %copy-start.19 = (s32[8]{0:T(128)S(1)}, s32[8]{0:T(128)}, u32[]{:S(2)}) copy-start(s32[8]{0:T(128)} %param.14) | copy-start | bytes 100
  0.6 12.5 %copy-start.16 = (f32[8,2048]{1,0:T(8,128)S(1)}, f32[8,2048]{1,0:T(8,128)}, u32[]{:S(2)}) copy-start(f32[8,2048]{1,0:T(8,128)} %param.11) | copy-start | bytes 196612
  0.7 12.5 %copy-start.17 = (s32[8,2048]{1,0:T(8,128)S(1)}, s32[8,2048]{1,0:T(8,128)}, u32[]{:S(2)}) copy-start(s32[8,2048]{1,0:T(8,128)} %param.10) | copy-start | bytes 196612
  0.7 12.5 %copy-start.18 = (f32[8,2048]{1,0:T(8,128)S(1)}, f32[8,2048]{1,0:T(8,128)}, u32[]{:S(2)}) copy-start(f32[8,2048]{1,0:T(8,128)} %param.9) | copy-start | bytes 196612
  7.3 5.9 %copy-start = (bf16[8,2048,256]{2,1,0:T(8,128)(2,1)S(1)}, bf16[8,2048,256]{2,1,0:T(8,128)(2,1)}, u32[]{:S(2)}) copy-start(bf16[8,2048,256]{2,1,0:T(8,128)(2,1)} %param.8) | copy-start | bytes 25165828
  15.0 25.4 %copy-start.20 = (s32[256]{0:T(256)S(1)}, s32[256]{0:T(256)}, u32[]{:S(2)}) copy-start(s32[256]{0:T(256)} %param.15) | copy-start | bytes 3076
  29.8 7.4 %collective-permute-start = (f32[4,35,8,128]{3,2,1,0:T(8,128)}, f32[4,35,8,128]{3,2,1,0:T(8,128)S(1)}, u32[]{:S(2)}, u32[]{:S(2)}) collective-permute-start(f32[4,35,8,128]{3,2,1,0:T(8,128)} %get-tuple-element.8), channel_id=1, source_target_pairs={{0,1},{1,0},{2,3},{3,2},{4,5},{5,4},{6,7},{7,6},{8,9},{9,8},{10,11... | collective-permute-start | bytes 1720328 | tf_op jit(solution)/shard_map/ppermute | solution.py:248
  38.4 5.4 %collective-permute-start.3 = (f32[35,8,128]{2,1,0:T(8,128)S(1)}, f32[35,8,128]{2,1,0:T(8,128)S(1)}, u32[]{:S(2)}, u32[]{:S(2)}) collective-permute-start(f32[35,8,128]{2,1,0:T(8,128)S(1)} %get-tuple-element.29), channel_id=1, source_target_pairs={{0,6},{1,7},{2,0},{3,1},{4,2},{5,3},{6,4},{7,5},{8,14},{9,15},{10,... | collective-permute-start | bytes 430088 | tf_op jit(solution)/shard_map/ppermute | solution.py:250
  39.3 6.6 %collective-permute-start.2 = (f32[35,8,128]{2,1,0:T(8,128)S(1)}, f32[35,8,128]{2,1,0:T(8,128)S(1)}, u32[]{:S(2)}, u32[]{:S(2)}) collective-permute-start(f32[35,8,128]{2,1,0:T(8,128)S(1)} %get-tuple-element.30), channel_id=1, source_target_pairs={{0,4},{1,5},{2,6},{3,7},{4,0},{5,1},{6,2},{7,3},{8,12},{9,13},{10,... | collective-permute-start | bytes 430088 | tf_op jit(solution)/shard_map/ppermute | solution.py:250
  39.8 9.7 %collective-permute-start.1 = (f32[35,8,128]{2,1,0:T(8,128)S(1)}, f32[35,8,128]{2,1,0:T(8,128)S(1)}, u32[]{:S(2)}, u32[]{:S(2)}) collective-permute-start(f32[35,8,128]{2,1,0:T(8,128)S(1)} %get-tuple-element.31), channel_id=1, source_target_pairs={{0,2},{1,3},{2,4},{3,5},{4,6},{5,7},{6,0},{7,1},{8,10},{9,11},{10,... | collective-permute-start | bytes 430088 | tf_op jit(solution)/shard_map/ppermute | solution.py:250
  49.6 9.5 %collective-permute-start.18 = (f32[17,8,128]{2,1,0:T(8,128)S(1)}, f32[17,8,128]{2,1,0:T(8,128)S(1)}, u32[]{:S(2)}, u32[]{:S(2)}) collective-permute-start(f32[17,8,128]{2,1,0:T(8,128)S(1)} %get-tuple-element.19), channel_id=1, source_target_pairs={{0,56},{8,0},{16,8},{24,16},{32,24},{40,32},{48,40},{56,48},{64,12... | collective-permute-start | bytes 208904 | tf_op jit(solution)/shard_map/ppermute | solution.py:29
  55.2 6.6 %collective-permute-start.14 = (f32[17,8,128]{2,1,0:T(8,128)S(1)}, f32[17,8,128]{2,1,0:T(8,128)S(1)}, u32[]{:S(2)}, u32[]{:S(2)}) collective-permute-start(f32[17,8,128]{2,1,0:T(8,128)S(1)} %get-tuple-element.19), channel_id=1, source_target_pairs={{0,8},{8,16},{16,24},{24,32},{32,40},{40,48},{48,56},{56,0},{64,72... | collective-permute-start | bytes 208904 | tf_op jit(solution)/shard_map/ppermute | solution.py:29
  55.2 6.5 %collective-permute-start.6 = (f32[18,8,128]{2,1,0:T(8,128)S(1)}, f32[18,8,128]{2,1,0:T(8,128)S(1)}, u32[]{:S(2)}, u32[]{:S(2)}) collective-permute-start(f32[18,8,128]{2,1,0:T(8,128)S(1)} %slice_add_fusion.4), channel_id=1, source_target_pairs={{0,192},{8,200},{16,208},{24,216},{32,224},{40,232},{48,240},{56,2... | collective-permute-start | bytes 221192 | tf_op jit(solution)/shard_map/ppermute | solution.py:29
  58.0 4.8 %collective-permute-start.5 = (f32[18,8,128]{2,1,0:T(8,128)S(1)}, f32[18,8,128]{2,1,0:T(8,128)S(1)}, u32[]{:S(2)}, u32[]{:S(2)}) collective-permute-start(f32[18,8,128]{2,1,0:T(8,128)S(1)} %slice_add_fusion.4), channel_id=1, source_target_pairs={{0,128},{8,136},{16,144},{24,152},{32,160},{40,168},{48,176},{56,1... | collective-permute-start | bytes 221192 | tf_op jit(solution)/shard_map/ppermute | solution.py:29
  58.4 5.5 %collective-permute-start.4 = (f32[18,8,128]{2,1,0:T(8,128)S(1)}, f32[18,8,128]{2,1,0:T(8,128)S(1)}, u32[]{:S(2)}, u32[]{:S(2)}) collective-permute-start(f32[18,8,128]{2,1,0:T(8,128)S(1)} %slice_add_fusion.4), channel_id=1, source_target_pairs={{0,64},{8,72},{16,80},{24,88},{32,96},{40,104},{48,112},{56,120},{... | collective-permute-start | bytes 221192 | tf_op jit(solution)/shard_map/ppermute | solution.py:29
  59.1 7.2 %collective-permute-start.19 = (f32[17,8,128]{2,1,0:T(8,128)S(1)}, f32[17,8,128]{2,1,0:T(8,128)S(1)}, u32[]{:S(2)}, u32[]{:S(2)}) collective-permute-start(f32[17,8,128]{2,1,0:T(8,128)S(1)} %collective-permute-done.18), channel_id=1, source_target_pairs={{0,56},{8,0},{16,8},{24,16},{32,24},{40,32},{48,40},{56,48},{64,12... | collective-permute-start | bytes 208904 | tf_op jit(solution)/shard_map/ppermute | solution.py:29
  61.8 7.2 %collective-permute-start.15 = (f32[17,8,128]{2,1,0:T(8,128)S(1)}, f32[17,8,128]{2,1,0:T(8,128)S(1)}, u32[]{:S(2)}, u32[]{:S(2)}) collective-permute-start(f32[17,8,128]{2,1,0:T(8,128)S(1)} %collective-permute-done.14), channel_id=1, source_target_pairs={{0,8},{8,16},{16,24},{24,32},{32,40},{40,48},{48,56},{56,0},{64,72... | collective-permute-start | bytes 208904 | tf_op jit(solution)/shard_map/ppermute | solution.py:29
  63.9 40.8 %copy-start.1 = (f32[72,8,128]{2,1,0:T(8,128)}, f32[72,8,128]{2,1,0:T(8,128)S(1)}, u32[]{:S(2)}) copy-start(f32[72,8,128]{2,1,0:T(8,128)S(1)} %pad_maximum_fusion.refs_0_) | copy-start | bytes 884740
  63.9 16.5 %collective-permute-start.11 = (f32[72,8,128]{2,1,0:T(8,128)S(1)}, f32[72,8,128]{2,1,0:T(8,128)S(1)}, u32[]{:S(2)}, u32[]{:S(2)}) collective-permute-start(f32[72,8,128]{2,1,0:T(8,128)S(1)} %pad_maximum_fusion.refs_0_), channel_id=1, source_target_pairs={{0,56},{8,0},{16,8},{24,16},{32,24},{40,32},{48,40},{56,48},{64,12... | collective-permute-start | bytes 884744 | tf_op jit(solution)/shard_map/ppermute | solution.py:29
  66.3 14.0 %collective-permute-start.7 = (f32[72,8,128]{2,1,0:T(8,128)S(1)}, f32[72,8,128]{2,1,0:T(8,128)S(1)}, u32[]{:S(2)}, u32[]{:S(2)}) collective-permute-start(f32[72,8,128]{2,1,0:T(8,128)S(1)} %pad_maximum_fusion.refs_0_), channel_id=1, source_target_pairs={{0,8},{8,16},{16,24},{24,32},{32,40},{40,48},{48,56},{56,0},{64,72... | collective-permute-start | bytes 884744 | tf_op jit(solution)/shard_map/ppermute | solution.py:29
  66.3 12.9 %collective-permute-start.20 = (f32[17,8,128]{2,1,0:T(8,128)S(1)}, f32[17,8,128]{2,1,0:T(8,128)S(1)}, u32[]{:S(2)}, u32[]{:S(2)}) collective-permute-start(f32[17,8,128]{2,1,0:T(8,128)S(1)} %collective-permute-done.19), channel_id=1, source_target_pairs={{0,56},{8,0},{16,8},{24,16},{32,24},{40,32},{48,40},{56,48},{64,12... | collective-permute-start | bytes 208904 | tf_op jit(solution)/shard_map/ppermute | solution.py:29
  69.0 5.8 %collective-permute-start.16 = (f32[17,8,128]{2,1,0:T(8,128)S(1)}, f32[17,8,128]{2,1,0:T(8,128)S(1)}, u32[]{:S(2)}, u32[]{:S(2)}) collective-permute-start(f32[17,8,128]{2,1,0:T(8,128)S(1)} %collective-permute-done.15), channel_id=1, source_target_pairs={{0,8},{8,16},{16,24},{24,32},{32,40},{40,48},{48,56},{56,0},{64,72... | collective-permute-start | bytes 208904 | tf_op jit(solution)/shard_map/ppermute | solution.py:29
  74.8 4.4 %collective-permute-start.17 = (f32[17,8,128]{2,1,0:T(8,128)S(1)}, f32[17,8,128]{2,1,0:T(8,128)S(1)}, u32[]{:S(2)}, u32[]{:S(2)}) collective-permute-start(f32[17,8,128]{2,1,0:T(8,128)S(1)} %collective-permute-done.16), channel_id=1, source_target_pairs={{0,8},{8,16},{16,24},{24,32},{32,40},{40,48},{48,56},{56,0},{64,72... | collective-permute-start | bytes 208904 | tf_op jit(solution)/shard_map/ppermute | solution.py:29
  79.3 25.5 %copy-start.2 = (f32[136,8,128]{2,1,0:T(8,128)}, f32[136,8,128]{2,1,0:T(8,128)S(1)}, u32[]{:S(2)}) copy-start(f32[136,8,128]{2,1,0:T(8,128)S(1)} %constant_dynamic-update-slice_fusion.refs_8_) | copy-start | bytes 1671172
  79.3 10.7 %collective-permute-start.21 = (f32[136,8,128]{2,1,0:T(8,128)S(1)}, f32[136,8,128]{2,1,0:T(8,128)S(1)}, u32[]{:S(2)}, u32[]{:S(2)}) collective-permute-start(f32[136,8,128]{2,1,0:T(8,128)S(1)} %constant_dynamic-update-slice_fusion.refs_8_), channel_id=1, source_target_pairs={{0,64},{8,72},{16,80},{24,88},{32,96},{40,104},{48,112},{56,120},{... | collective-permute-start | bytes 1671176 | tf_op jit(solution)/shard_map/ppermute | solution.py:29
  80.4 24.4 %copy-start.7 = (f32[72,8,128]{2,1,0:T(8,128)}, f32[72,8,128]{2,1,0:T(8,128)S(1)}, u32[]{:S(2)}) copy-start(f32[72,8,128]{2,1,0:T(8,128)S(1)} %collective-permute-done.7.refs_1_) | copy-start | bytes 884740
  80.4 6.8 %collective-permute-start.8 = (f32[72,8,128]{2,1,0:T(8,128)S(1)}, f32[72,8,128]{2,1,0:T(8,128)S(1)}, u32[]{:S(2)}, u32[]{:S(2)}) collective-permute-start(f32[72,8,128]{2,1,0:T(8,128)S(1)} %collective-permute-done.7.refs_1_), channel_id=1, source_target_pairs={{0,8},{8,16},{16,24},{24,32},{32,40},{40,48},{48,56},{56,0},{64,72... | collective-permute-start | bytes 884744 | tf_op jit(solution)/shard_map/ppermute | solution.py:29
  80.5 24.3 %copy-start.6 = (f32[72,8,128]{2,1,0:T(8,128)}, f32[72,8,128]{2,1,0:T(8,128)S(1)}, u32[]{:S(2)}) copy-start(f32[72,8,128]{2,1,0:T(8,128)S(1)} %collective-permute-done.11.refs_7_) | copy-start | bytes 884740
  80.5 10.0 %collective-permute-start.12 = (f32[72,8,128]{2,1,0:T(8,128)S(1)}, f32[72,8,128]{2,1,0:T(8,128)}, u32[]{:S(2)}, u32[]{:S(2)}) collective-permute-start(f32[72,8,128]{2,1,0:T(8,128)S(1)} %collective-permute-done.11.refs_7_), channel_id=1, source_target_pairs={{0,56},{8,0},{16,8},{24,16},{32,24},{40,32},{48,40},{56,48},{64,12... | collective-permute-start | bytes 884744 | tf_op jit(solution)/shard_map/ppermute | solution.py:29
  87.2 17.7 %copy-start.8 = (f32[72,8,128]{2,1,0:T(8,128)}, f32[72,8,128]{2,1,0:T(8,128)S(1)}, u32[]{:S(2)}) copy-start(f32[72,8,128]{2,1,0:T(8,128)S(1)} %collective-permute-done.8.refs_2_) | copy-start | bytes 884740
  87.2 8.4 %collective-permute-start.9 = (f32[72,8,128]{2,1,0:T(8,128)S(1)}, f32[72,8,128]{2,1,0:T(8,128)}, u32[]{:S(2)}, u32[]{:S(2)}) collective-permute-start(f32[72,8,128]{2,1,0:T(8,128)S(1)} %collective-permute-done.8.refs_2_), channel_id=1, source_target_pairs={{0,8},{8,16},{16,24},{24,32},{32,40},{40,48},{48,56},{56,0},{64,72... | collective-permute-start | bytes 884744 | tf_op jit(solution)/shard_map/ppermute | solution.py:29
  87.2 9.0 %collective-permute-start.23 = (f32[136,8,128]{2,1,0:T(8,128)S(1)}, f32[136,8,128]{2,1,0:T(8,128)S(1)}, u32[]{:S(2)}, u32[]{:S(2)}) collective-permute-start(f32[136,8,128]{2,1,0:T(8,128)S(1)} %constant_dynamic-update-slice_fusion.refs_8_), channel_id=1, source_target_pairs={{0,192},{8,200},{16,208},{24,216},{32,224},{40,232},{48,240},{56,2... | collective-permute-start | bytes 1671176 | tf_op jit(solution)/shard_map/ppermute | solution.py:29
  90.0 14.8 %copy-start.3 = (f32[136,8,128]{2,1,0:T(8,128)}, f32[136,8,128]{2,1,0:T(8,128)S(1)}, u32[]{:S(2)}) copy-start(f32[136,8,128]{2,1,0:T(8,128)S(1)} %collective-permute-done.21.refs_9_) | copy-start | bytes 1671172
  90.0 14.8 %collective-permute-start.22 = (f32[136,8,128]{2,1,0:T(8,128)S(1)}, f32[136,8,128]{2,1,0:T(8,128)S(1)}, u32[]{:S(2)}, u32[]{:S(2)}) collective-permute-start(f32[136,8,128]{2,1,0:T(8,128)S(1)} %collective-permute-done.21.refs_9_), channel_id=1, source_target_pairs={{0,64},{8,72},{16,80},{24,88},{32,96},{40,104},{48,112},{56,120},{... | collective-permute-start | bytes 1671176 | tf_op jit(solution)/shard_map/ppermute | solution.py:29
  90.5 6.0 %collective-permute-start.13 = (f32[72,8,128]{2,1,0:T(8,128)}, f32[72,8,128]{2,1,0:T(8,128)}, u32[]{:S(2)}, u32[]{:S(2)}) collective-permute-start(f32[72,8,128]{2,1,0:T(8,128)} %collective-permute-done.12.refs_6_), channel_id=1, source_target_pairs={{0,56},{8,0},{16,8},{24,16},{32,24},{40,32},{48,40},{56,48},{64,12... | collective-permute-start | bytes 884744 | tf_op jit(solution)/shard_map/ppermute | solution.py:29
  95.5 9.2 %collective-permute-start.10 = (f32[72,8,128]{2,1,0:T(8,128)}, f32[72,8,128]{2,1,0:T(8,128)}, u32[]{:S(2)}, u32[]{:S(2)}) collective-permute-start(f32[72,8,128]{2,1,0:T(8,128)} %collective-permute-done.9.refs_3_), channel_id=1, source_target_pairs={{0,8},{8,16},{16,24},{24,32},{32,40},{40,48},{48,56},{56,0},{64,72... | collective-permute-start | bytes 884744 | tf_op jit(solution)/shard_map/ppermute | solution.py:29
  96.2 8.6 %copy-start.4 = (f32[136,8,128]{2,1,0:T(8,128)}, f32[136,8,128]{2,1,0:T(8,128)S(1)}, u32[]{:S(2)}) copy-start(f32[136,8,128]{2,1,0:T(8,128)S(1)} %collective-permute-done.23.refs_11_) | copy-start | bytes 1671172
  104.8 0.8 copy-start.5
  111.8 14.6 %collective-permute-start.26 = (f32[16,16,128]{2,1,0:T(8,128)S(1)}, f32[16,16,128]{2,1,0:T(8,128)S(1)}, u32[]{:S(2)}, u32[]{:S(2)}) collective-permute-start(f32[16,16,128]{2,1,0:T(8,128)S(1)} %get-tuple-element.36), channel_id=1, source_target_pairs={{0,6},{1,7},{2,0},{3,1},{4,2},{5,3},{6,4},{7,5},{8,14},{9,15},{10,... | collective-permute-start | bytes 393224 | tf_op jit(solution)/shard_map/ppermute | solution.py:303
  112.3 15.2 %collective-permute-start.25 = (f32[16,16,128]{2,1,0:T(8,128)S(1)}, f32[16,16,128]{2,1,0:T(8,128)S(1)}, u32[]{:S(2)}, u32[]{:S(2)}) collective-permute-start(f32[16,16,128]{2,1,0:T(8,128)S(1)} %get-tuple-element.37), channel_id=1, source_target_pairs={{0,4},{1,5},{2,6},{3,7},{4,0},{5,1},{6,2},{7,3},{8,12},{9,13},{10,... | collective-permute-start | bytes 393224 | tf_op jit(solution)/shard_map/ppermute | solution.py:303
  112.8 16.1 %collective-permute-start.24 = (f32[16,16,128]{2,1,0:T(8,128)S(1)}, f32[16,16,128]{2,1,0:T(8,128)S(1)}, u32[]{:S(2)}, u32[]{:S(2)}) collective-permute-start(f32[16,16,128]{2,1,0:T(8,128)S(1)} %get-tuple-element.38), channel_id=1, source_target_pairs={{0,2},{1,3},{2,4},{3,5},{4,6},{5,7},{6,0},{7,1},{8,10},{9,11},{10,... | collective-permute-start | bytes 393224 | tf_op jit(solution)/shard_map/ppermute | solution.py:303
  114.4 14.6 %collective-permute-start.30 = (f32[16,16,128]{2,1,0:T(8,128)S(1)}, f32[16,16,128]{2,1,0:T(8,128)S(1)}, u32[]{:S(2)}, u32[]{:S(2)}) collective-permute-start(f32[16,16,128]{2,1,0:T(8,128)S(1)} %get-tuple-element.32), channel_id=1, source_target_pairs={{0,7},{1,6},{2,1},{3,0},{4,3},{5,2},{6,5},{7,4},{8,15},{9,14},{10,... | collective-permute-start | bytes 393224 | tf_op jit(solution)/shard_map/ppermute | solution.py:304
  125.4 6.7 %collective-permute-start.29 = (f32[16,16,128]{2,1,0:T(8,128)S(1)}, f32[16,16,128]{2,1,0:T(8,128)S(1)}, u32[]{:S(2)}, u32[]{:S(2)}) collective-permute-start(f32[16,16,128]{2,1,0:T(8,128)S(1)} %get-tuple-element.33), channel_id=1, source_target_pairs={{0,5},{1,4},{2,7},{3,6},{4,1},{5,0},{6,3},{7,2},{8,13},{9,12},{10,... | collective-permute-start | bytes 393224 | tf_op jit(solution)/shard_map/ppermute | solution.py:304
  126.5 8.3 %copy-start.9 = (f32[16,16,128]{2,1,0:T(8,128)}, f32[16,16,128]{2,1,0:T(8,128)S(1)}, u32[]{:S(2)}) copy-start(f32[16,16,128]{2,1,0:T(8,128)S(1)} %collective-permute-done.26) | copy-start | bytes 393220
  126.5 8.3 %collective-permute-start.28 = (f32[16,16,128]{2,1,0:T(8,128)S(1)}, f32[16,16,128]{2,1,0:T(8,128)S(1)}, u32[]{:S(2)}, u32[]{:S(2)}) collective-permute-start(f32[16,16,128]{2,1,0:T(8,128)S(1)} %get-tuple-element.34), channel_id=1, source_target_pairs={{0,3},{1,2},{2,5},{3,4},{4,7},{5,6},{6,1},{7,0},{8,11},{9,10},{10,... | collective-permute-start | bytes 393224 | tf_op jit(solution)/shard_map/ppermute | solution.py:304
  127.5 7.3 %copy-start.10 = (f32[16,16,128]{2,1,0:T(8,128)}, f32[16,16,128]{2,1,0:T(8,128)S(1)}, u32[]{:S(2)}) copy-start(f32[16,16,128]{2,1,0:T(8,128)S(1)} %collective-permute-done.25) | copy-start | bytes 393220
  127.5 7.3 %collective-permute-start.27 = (f32[16,16,128]{2,1,0:T(8,128)S(1)}, f32[16,16,128]{2,1,0:T(8,128)S(1)}, u32[]{:S(2)}, u32[]{:S(2)}) collective-permute-start(f32[16,16,128]{2,1,0:T(8,128)S(1)} %get-tuple-element.35), channel_id=1, source_target_pairs={{0,1},{1,0},{2,3},{3,2},{4,5},{5,4},{6,7},{7,6},{8,9},{9,8},{10,11... | collective-permute-start | bytes 393224 | tf_op jit(solution)/shard_map/ppermute | solution.py:304
  128.8 6.0 %copy-start.11 = (f32[16,16,128]{2,1,0:T(8,128)}, f32[16,16,128]{2,1,0:T(8,128)S(1)}, u32[]{:S(2)}) copy-start(f32[16,16,128]{2,1,0:T(8,128)S(1)} %collective-permute-done.24) | copy-start | bytes 393220
  129.0 5.8 %copy-start.12 = (f32[16,16,128]{2,1,0:T(8,128)}, f32[16,16,128]{2,1,0:T(8,128)S(1)}, u32[]{:S(2)}) copy-start(f32[16,16,128]{2,1,0:T(8,128)S(1)} %collective-permute-done.30) | copy-start | bytes 393220
  132.1 2.7 %copy-start.13 = (f32[16,16,128]{2,1,0:T(8,128)}, f32[16,16,128]{2,1,0:T(8,128)S(1)}, u32[]{:S(2)}) copy-start(f32[16,16,128]{2,1,0:T(8,128)S(1)} %collective-permute-done.29) | copy-start | bytes 393220
  134.8 0.6 copy-start.14
  134.8 0.7 copy-start.15

commit v2 on v1

v2 whole, which is shorter than its diff:
```python
import functools

import jax
import jax.numpy as jnp
from jax import lax
from jax.experimental import pallas as pl
from jax.experimental.pallas import tpu as pltpu
from jax.sharding import PartitionSpec as P

GW = 128
TILE = 512
NY, NZ, NX, NC = 4, 8, 4, 2
QA, QB = 18, 17
F32, BF16 = jnp.float32, jnp.bfloat16


def z_shift(s):
    return [(y * NZ + z, y * NZ + (z + s) % NZ) for y in range(NY) for z in range(NZ)]


def y_shift(s):
    return [(y * NZ + z, (y + s) % NY * NZ + z) for y in range(NY) for z in range(NZ)]


def x_shift(s, flip):
    return [(x * NC + c, (x + s) % NX * NC + (c ^ flip)) for x in range(NX) for c in range(NC)]


def on_chan(value, perm):
    return lax.ppermute(value, "chan", perm)


def gather_a(own):
    near = [own] + [on_chan(own, y_shift(d)) for d in (1, 2, 3)]
    held = jnp.concatenate(near, axis=0)
    up, down = held, held
    found = {0: held}
    for s in (1, 2, 3):
        up, down = on_chan(up, z_shift(1)), on_chan(down, z_shift(-1))
        found[s], found[NZ - s] = up, down
    half = NY // 2
    far = (on_chan(up[: half * QA], z_shift(1)), on_chan(down[half * QA :], z_shift(-1)))
    where = {(dy, dz): (found[dz], dy * QA) for dy in range(NY) for dz in range(NZ) if dz != 4}
    where.update({(dy, 4): (far[dy // half], dy % half * QA) for dy in range(NY)})
    return where


def gather_b(own):
    near = {0: own}
    for d in (1, 2, -2, -1):
        near[d % NZ] = on_chan(own, z_shift(d))
    near[3] = on_chan(near[2], z_shift(1))
    near[4] = on_chan(near[2], z_shift(2))
    near[5] = on_chan(near[6], z_shift(-1))
    held = jnp.concatenate([near[d] for d in range(NZ)], axis=0)
    up, down = on_chan(held, y_shift(1)), on_chan(held, y_shift(-1))
    half = NZ // 2
    far = (on_chan(up[: half * QB], y_shift(1)), on_chan(down[half * QB :], y_shift(-1)))
    found = {0: held, 1: up, 3: down}
    where = {(dy, dz): (found[dy], dz * QB) for dy in (0, 1, 3) for dz in range(NZ)}
    where.update({(2, dz): (far[dz // half], dz % half * QB) for dz in range(NZ)})
    return where


def here(device):
    bins_index = lax.rem(device, NX * NC)
    return lax.div(bins_index, NC), lax.rem(bins_index, NC), bins_index


def bins_kernel(
    device_ref, index_ref, counts_ref, theta_ref, nominal_ref, observed_ref, variance_ref, effects_ref,
    mine_ref, other_ref, a_ref, o_ref, b_ref, g_ref,
):
    c = pl.program_id(0)
    x, core, bins_index = here(device_ref[0])
    count = effects_ref.shape[1]
    effects = effects_ref[0]
    chosen = jnp.concatenate(
        [theta_ref[pl.ds(lax.div(index_ref[c, k * GW], GW), 1), :] for k in range(2)], axis=1
    )
    chosen = jnp.broadcast_to(chosen, (8, 2 * GW)).astype(BF16)
    exponent = lax.dot_general(chosen, effects, (((1,), (1,)), ((), ())), preferred_element_type=F32)[:1]
    expected = nominal_ref[pl.ds(c, 1), :] * jnp.exp(exponent)
    denominator = 1.0 + expected * variance_ref[pl.ds(c, 1), :]
    positions = bins_index * count + lax.broadcasted_iota(jnp.int32, (1, count), 1)
    live = positions < counts_ref[c]
    residual = jnp.where(
        live, (expected - observed_ref[pl.ds(c, 1), :].astype(F32)) / denominator, 0.0
    )
    root = jnp.sqrt(jnp.where(live, expected / denominator, 0.0))
    g_ref[pl.ds(c, 1), :] = jnp.dot(
        jnp.broadcast_to(residual, (8, count)).astype(BF16), effects, preferred_element_type=F32
    )[:1]
    column = jnp.broadcast_to(root, (GW, count)).T
    scaled = (jnp.concatenate([column, column], axis=1) * effects.astype(F32)).astype(BF16)
    left, right = scaled[:, :GW], scaled[:, GW:]

    both = lax.dot_general(left, scaled, (((0,), (0,)), ((), ())), preferred_element_type=F32)
    rows = pl.ds(pl.multiple_of(c * GW, GW), GW)
    a_ref[rows, :] = both[:, :GW]
    o_ref[rows, :] = both[:, GW:]
    b_ref[rows, :] = lax.dot_general(right, right, (((0,), (0,)), ((), ())), preferred_element_type=F32)

    @pl.when(c == pl.num_programs(0) - 1)
    def _():
        lane = lax.broadcasted_iota(jnp.int32, (8, GW), 1)
        diag = jnp.zeros((8, GW), F32)
        for row in range(GW):
            diag = jnp.where(lane == row, a_ref[pl.ds(row, 8, stride=GW), :], diag)
        grads = g_ref[...]
        for d in range(NX):
            for ref, side in ((mine_ref, core), (other_ref, 1 - core)):
                start = lax.rem(x + d, NX) * 32 + side * 16
                for q in range(16):
                    row = start + q
                    ref[d, q] = o_ref[pl.ds(row, 8, stride=GW), :]
                    a = a_ref[pl.ds(row, 8, stride=GW), :]
                    b = b_ref[pl.ds(row, 8, stride=GW), :]
                    ref[d, QA + q] = jnp.where(lane > row, a, b)
                ref[d, 16] = grads[:, :GW]
                ref[d, 17] = grads[:, GW:]
                ref[d, QA + 16] = diag


def split2(v):
    high = v.astype(BF16)
    return high, (v - high.astype(F32)).astype(BF16)


def place_kernel(arrays, offsets_a, offsets_b, device_ref, meta_ref, *refs):
    ins, outs, grad_ref = refs[:arrays], refs[arrays:-1], refs[-1]
    slice_index = here(device_ref[0])[2]
    pos = lax.broadcasted_iota(jnp.int32, (128, 256), 0)
    meta = meta_ref[...]

    def hot(*rows):
        hit = pos == meta[rows[0] : rows[0] + 1]
        for r in rows[1:]:
            hit = jnp.logical_or(hit, pos == meta[r : r + 1])
        return jnp.where(hit, 1.0, 0.0).astype(BF16)

    sel_off = hot(0, 1)
    sel_both = jnp.concatenate([hot(2), hot(3)], axis=0)
    lane = lax.broadcasted_iota(jnp.int32, (128, GW), 1)

    def gathered(offsets, q):
        return jnp.concatenate([ins[k][o + q] for k, o in offsets], axis=0)

    def apply(sel, v):
        high, low = split2(v)
        return jnp.dot(sel, high, preferred_element_type=F32) + jnp.dot(
            sel, low, preferred_element_type=F32
        )

    diag = apply(sel_both[:128], gathered(offsets_b, 16))
    grads = apply(hot(4)[:8], gathered(offsets_a, 16)) + apply(hot(5)[:8], gathered(offsets_a, 17))
    grad_ref[...] = grads
    for q in range(0, 16, 2):
        off = apply(
            sel_off, jnp.concatenate([gathered(offsets_a, q), gathered(offsets_a, q + 1)], axis=1)
        )
        both = apply(
            sel_both, jnp.concatenate([gathered(offsets_b, q), gathered(offsets_b, q + 1)], axis=1)
        )
        for k in range(2):
            row = slice_index * 16 + q + k
            cols = slice(k * GW, (k + 1) * GW)
            upper, lower = both[:128, cols], both[128:, cols]
            value = off[:, cols] + jnp.where(lane > row, upper, lower)
            value = value + jnp.where(lane == row, diag, 0.0)
            for k_out in range(NX * NC):
                outs[k_out][q + k] = value[k_out * 16 : (k_out + 1) * 16]


def finish_kernel(tile_side, device_ref, owner_ref, *refs):
    ins, out_ref, tile_ref = refs[:8], refs[8], refs[9]
    x, core, _ = here(device_ref[0])
    tile = owner_ref[device_ref[0]]
    tile_row, tile_col = lax.div(tile, tile_side), lax.rem(tile, tile_side)
    k = 0
    for flip in range(NC):
        for d in range(NX):
            source = lax.rem(x - d + NX, NX) * 2 + (core + flip) % 2
            for rc in range(16):
                start = pl.multiple_of(source * 16 + rc // 4 * GW, 16)
                tile_ref[pl.ds(start, 16), rc % 4 * GW : (rc % 4 + 1) * GW] = ins[k][
                    pl.ds(rc, 16, stride=16), :
                ]
            k += 1

    @pl.when(tile_row < tile_col)
    def _():
        out_ref[0] = tile_ref[...]

    @pl.when(tile_row > tile_col)
    def _():
        for r in range(4):
            for c in range(4):
                out_ref[0, r * GW : (r + 1) * GW, c * GW : (c + 1) * GW] = tile_ref[
                    c * GW : (c + 1) * GW, r * GW : (r + 1) * GW
                ].T

    @pl.when(tile_row == tile_col)
    def _():
        row = lax.broadcasted_iota(jnp.int32, (GW, GW), 0)
        col = lax.broadcasted_iota(jnp.int32, (GW, GW), 1)
        for r in range(4):
            for c in range(4):
                here = tile_ref[r * GW : (r + 1) * GW, c * GW : (c + 1) * GW]
                there = tile_ref[c * GW : (c + 1) * GW, r * GW : (r + 1) * GW].T
                value = here + there
                if r == c:
                    value = jnp.where(row == col, here + 1.0, value)
                out_ref[0, r * GW : (r + 1) * GW, c * GW : (c + 1) * GW] = value


VMEM = pl.BlockSpec(memory_space=pltpu.VMEM)
SMEM = pl.BlockSpec(memory_space=pltpu.SMEM)


def shape(*dims):
    return jax.ShapeDtypeStruct(dims, F32)


def cost(flops, moved):
    return pl.CostEstimate(flops=flops, bytes_accessed=moved, transcendentals=0)


def local(effects, nominal, observed, mc_variance, theta, nuisance_index, bin_counts, tile_owner):
    chan_index, bins_index = lax.axis_index("chan"), lax.axis_index("bins")
    y, z, x, core = chan_index // NZ, chan_index % NZ, bins_index // NC, bins_index % NC
    chans, bins, width = effects.shape
    tile_side = theta.shape[0] // TILE
    slot = chan_index * (NX * NC) + bins_index
    device = slot.astype(jnp.int32).reshape(1)

    tiles = QA + QB
    mine, other = pl.pallas_call(
        bins_kernel,
        grid_spec=pltpu.PrefetchScalarGridSpec(
            num_scalar_prefetch=1,
            grid=(chans,),
            in_specs=[
                pl.BlockSpec(
                    (chans, width), lambda c, d: (lax.div(d[0], NX * NC), 0), memory_space=pltpu.SMEM
                ),
                SMEM,
                VMEM,
                VMEM,
                VMEM,
                VMEM,
                pl.BlockSpec((1, bins, width), lambda c, d: (c, 0, 0)),
            ],
            out_specs=[VMEM] * 2,
            scratch_shapes=[pltpu.VMEM((8 * GW, GW), F32)] * 3 + [pltpu.VMEM((8, width), F32)],
        ),
        out_shape=[shape(NX, tiles, 8, GW)] * 2,
        compiler_params=pltpu.CompilerParams(dimension_semantics=("arbitrary",)),
        cost_estimate=cost(2 * 10**9, 12 * 10**6),
        name="bins",
    )(device, nuisance_index, bin_counts, theta.reshape(-1, GW), nominal, observed, mc_variance, effects)
    other = lax.ppermute(other, "bins", x_shift(0, 1))
    chip = [mine[d] + other[d] for d in range(NX)]
    chip[1], nuisance_index, tile_owner = lax.optimization_barrier((chip[1], nuisance_index, tile_owner))
    arrived = [lax.ppermute(chip[d], "bins", x_shift(d, 0)) for d in (1, 2, 3)]
    own_a = chip[0][:QA] + arrived[0][:QA] + arrived[1][:QA] + arrived[2][:QA]
    own_b = chip[0][QA:] + arrived[0][QA:] + arrived[1][QA:] + arrived[2][QA:]

    at_a, at_b = gather_a(own_a), gather_b(own_b)
    order = [(dy, dz) for dy in range(NY) for dz in range(NZ)]
    arrays, offsets_a, offsets_b = [], [], []
    for at, offsets in ((at_a, offsets_a), (at_b, offsets_b)):
        for key in order:
            array, offset = at[key]
            known = [k for k, v in enumerate(arrays) if v is array]
            if not known:
                arrays.append(array)
                known = [len(arrays) - 1]
            offsets.append((known[0], offset))

    dy = jnp.arange(NY, dtype=jnp.int32)[:, None, None]
    dz = jnp.arange(NZ, dtype=jnp.int32)[None, :, None]
    channel = ((y - dy + NY) % NY * NZ + (z - dz + NZ) % NZ) * chans
    channel = (channel + jnp.arange(chans, dtype=jnp.int32)).reshape(-1)
    at = jnp.arange(channel.shape[0], dtype=jnp.int32)[:, None] == channel[None, :]
    first, second = [
        jnp.sum(jnp.where(at, nuisance_index[:, k * GW : k * GW + 1] // GW, 0), axis=0) for k in range(2)
    ]
    row_tiles = lax.dynamic_slice_in_dim(tile_owner, chan_index * 8, 8, 0)
    rel = (jnp.arange(8, dtype=jnp.int32) // NC - x + NX) % NX * NC + (jnp.arange(8, dtype=jnp.int32) + core) % NC
    per = TILE // GW

    def slot_of(tile_ids, inside):
        hit = row_tiles[:, None] == tile_ids[None, :]
        base = jnp.sum(jnp.where(hit, rel[:, None] * 16 + inside[None, :] + 1, 0), axis=0)
        return base - 1

    tr, tc = first // per, second // per
    inside = first % per * per + second % per
    straight = slot_of(tr * tile_side + tc, inside)
    mirrored = jnp.where(tr == tc, -1, slot_of(tc * tile_side + tr, inside))
    upper = slot_of(tr * (tile_side + 1), first % per * (per + 1))
    lower = slot_of(tc * (tile_side + 1), second % per * (per + 1))
    meta = jnp.stack(
        [straight, mirrored, upper, lower, first - 2 * chan_index, second - 2 * chan_index, upper, lower]
    )

    *dense, grad_rows = pl.pallas_call(
        functools.partial(place_kernel, len(arrays), offsets_a, offsets_b),
        out_shape=[shape(16, 16, GW)] * 8 + [shape(8, GW)],
        in_specs=[SMEM, VMEM] + [VMEM] * len(arrays),
        out_specs=[VMEM] * 9,
        cost_estimate=cost(10**9, 6 * 10**6),
        name="place",
    )(device, meta, *arrays)

    hops = {}
    for d in (2, 1, 3, 0):
        for flip in range(NC):
            v = dense[NC * d + flip]
            hops[flip, d] = lax.ppermute(v, "bins", x_shift(d, flip)) if d + flip else v
    ins = [hops[flip, d] for flip in range(NC) for d in range(NX)]
    hessian_tiles = pl.pallas_call(
        functools.partial(finish_kernel, tile_side),
        out_shape=shape(1, TILE, TILE),
        in_specs=[SMEM] * 2 + [VMEM] * 8,
        out_specs=VMEM,
        scratch_shapes=[pltpu.VMEM((TILE, TILE), F32)],
        cost_estimate=cost(10**6, 2 * 10**6),
        name="finish",
    )(device, tile_owner, *[v.reshape(256, GW) for v in ins])

    part = lax.dynamic_slice(
        grad_rows, (bins_index // 4, bins_index % 4 * 32), (1, 32)
    ).reshape(-1)
    gradient = part + lax.dynamic_slice_in_dim(theta, slot * 32, 32, 0)
    return hessian_tiles, gradient


def solution(mesh):
    return jax.shard_map(
        local,
        mesh=mesh,
        in_specs=(
            P("chan", "bins", None),
            P("chan", "bins"),
            P("chan", "bins"),
            P("chan", "bins"),
            P(),
            P(),
            P("chan"),
            P(),
        ),
        out_specs=(P(("chan", "bins"), None, None), P(("chan", "bins"))),
        check_vma=False,
    )
```

time: 139 us -> 115 us (0.83)
  matrix products: 17.2 us -> 0 us
  waiting for transfers between devices: 44.8 us -> 30.5 us
  starting transfers between devices: 44.2 us -> 54.9 us
  local copies, waits for them, and re-layouts: 14.2 us -> 4.52 us
  Pallas kernels: 11.2 us -> 20.2 us
  between operations: 3.7 us -> 1.03 us
    dot_general x3 -> x0, matrix products: 17.2 us -> none  [the longest x1 10.2 us: local(): jnp.einsum('cbk,cbl->ckl', scaled, scaled, preferred_element_type=F32)]
    ppermute x20 -> x22, waiting for transfers between devices: 29.8 us -> 19.6 us  [on_chan(): return lax.ppermute(value, 'chan', perm)]
    pallas_call x2, Pallas kernels: 6.8 us -> 15.8 us  [the longest x1 12.9 us: local(): pl.pallas_call(bins_kernel, grid_spec=pltpu.PrefetchScalarGridSpec(num_sc...]
    ppermute x20 -> x22, starting transfers between devices: 24.5 us -> 30 us  [on_chan(): return lax.ppermute(value, 'chan', perm)]
    gather x3 -> x0, local copies, waits for them, and re-layouts: 5.22 us -> none  [the longest x2 3.89 us: local(): first, second = (groups[channel, 0], groups[channel, 1])]
    ppermute x7, starting transfers between devices: 14.5 us -> 18.9 us  [local(): hops[flip, d] = lax.ppermute(v, 'bins', x_shift(d, flip)) if d + flip else v]
    ppermute x3, waiting for transfers between devices: 9.03 us -> 5.6 us  [local(): arrived = [lax.ppermute(chip[d], 'bins', x_shift(d, 0)) for d in (1, 2, 3)]]
    squeeze x2 -> x0, local copies, waits for them, and re-layouts: 2.9 us -> none  [the longest x1 1.78 us: local(): mine[d]]
  transfers between devices with their start and end apart: 31 -> 33, of which waited for: 15 -> 15; matrix products, arithmetic and copies ran while one was open for 5% -> 5% of each run, Pallas kernels for 0% -> 0%
where the time goes in v2:
time: 115 us; the launch traced here: 114 us
  starting transfers between devices  54.9 us (48%)
  waiting for transfers between devices  30.5 us (27%)
  Pallas kernels  20.2 us (18%)
  local copies, waits for them, and re-layouts  4.52 us (4%)
  other arithmetic  3.24 us (3%)
    ppermute x22, starting transfers between devices, on_chan(): return lax.ppermute(value, 'chan', perm)  30 us
    ppermute x22, waiting for transfers between devices, on_chan(): return lax.ppermute(value, 'chan', perm)  19.6 us
    ppermute x7, starting transfers between devices, local(): hops[flip, d] = lax.ppermute(v, 'bins', x_shift(d, flip)) if d + flip else v  18.9 us
    pallas_call x1, Pallas kernels, local(): pl.pallas_call(bins_kernel, grid_spec=pltpu.PrefetchScalarGridSpec(num_sc...  12.9 us
    ppermute x3, waiting for transfers between devices, local(): arrived = [lax.ppermute(chip[d], 'bins', x_shift(d, 0)) for d in (1, 2, 3)]  5.6 us
    pallas_call x1, Pallas kernels, local(): pl.pallas_call(functools.partial(place_kernel, len(arrays), offsets_a, of...  4.39 us
    ppermute x7, waiting for transfers between devices, local(): hops[flip, d] = lax.ppermute(v, 'bins', x_shift(d, flip)) if d + flip else v  3.72 us
    ppermute x1, starting transfers between devices, local(): other = lax.ppermute(other, 'bins', x_shift(0, 1))  3.2 us
  transfers between devices with their start and end apart: 33, of which 15 were waited for; matrix products, arithmetic and copies ran while one was open for 5% of the time, Pallas kernels for 0%

profile of v2, /device:TPU:1, one launch (start us, length us, event | category | flops | bytes accessed | tf_op | source)
XLA Modules:
  0.0 114.3 jit_solution(6568016981850333323)
XLA Ops:
  0.6 0.0 copy-start.18
  0.7 12.9 %bins.1 = (f32[4,35,8,128]{3,2,1,0:T(8,128)}, f32[4,35,8,128]{3,2,1,0:T(8,128)}) custom-call(s32[1]{0:T(128)} %bitcast.device_ref, s32[256,256]{1,0:T(8,128)} %index_ref.1, s32[8]{0:T(128)} %counts_ref.1, f32[64,128]{1,0:T(8,128)} %bitcast.41, f32[8,2048]{1,0:T(8,128)} %nominal_ref.1, s32[8,2048]{1,0:T(8,128)} %observed_ref.1, f32[8,2048]{1,0:T(8,128)} %variance_ref.1, ...), custom_call_target="tpu_custom_call" | custom-call | flops 2000000000 | bytes 12000000 | tf_op jit(solution)/shard_map/bins/pallas_call | solution.py:238
  13.5 3.2 %collective-permute-start = (f32[4,35,8,128]{3,2,1,0:T(8,128)}, f32[4,35,8,128]{3,2,1,0:T(8,128)S(1)}, u32[]{:S(2)}, u32[]{:S(2)}) collective-permute-start(f32[4,35,8,128]{3,2,1,0:T(8,128)} %get-tuple-element.17), channel_id=1, source_target_pairs={{0,1},{1,0},{2,3},{3,2},{4,5},{5,4},{6,7},{7,6},{8,9},{9,8},{10,11... | collective-permute-start | bytes 1720328 | tf_op jit(solution)/shard_map/ppermute | solution.py:262
  16.8 0.1 add_multiply_fusion
  16.9 0.1 iota_add_fusion
  16.9 0.1 add.382
  17.1 1.5 %collective-permute-done = f32[4,35,8,128]{3,2,1,0:T(8,128)S(1)} collective-permute-done((f32[4,35,8,128]{3,2,1,0:T(8,128)}, f32[4,35,8,128]{3,2,1,0:T(8,128)S(1)}, u32[]{:S(2)}, u32[]{:S(2)}) %collective-permute-start) | collective-permute-done | bytes 573472 | tf_op jit(solution)/shard_map/ppermute | solution.py:262
  18.6 1.2 %slice_add_fusion.2 = (f32[1,35,8,128]{3,2,1,0:T(8,128)S(1)}, f32[35,8,128]{2,1,0:T(8,128)S(1)}, f32[35,8,128]{2,1,0:T(8,128)S(1)}, f32[35,8,128]{2,1,0:T(8,128)S(1)}) fusion(f32[4,35,8,128]{3,2,1,0:T(8,128)S(1)} %collective-permute-done, f32[4,35,8,128]{3,2,1,0:T(8,128)} %get-tuple-element.16), kind=kLoop, calls=%fused_computation.16 | loop fusion | flops 143360 | bytes 1720320 | tf_op jit(solution)/shard_map/add | solution.py:263
  19.7 0.2 fusion.4
  20.0 0.1 collective-permute-start.1
  20.1 2.7 %collective-permute-start.3 = (f32[35,8,128]{2,1,0:T(8,128)S(1)}, f32[35,8,128]{2,1,0:T(8,128)S(1)}, u32[]{:S(2)}, u32[]{:S(2)}) collective-permute-start(f32[35,8,128]{2,1,0:T(8,128)S(1)} %get-tuple-element.49), channel_id=1, source_target_pairs={{0,6},{1,7},{2,0},{3,1},{4,2},{5,3},{6,4},{7,5},{8,14},{9,15},{10,... | collective-permute-start | bytes 430088 | tf_op jit(solution)/shard_map/ppermute | solution.py:265
  22.7 0.0 collective-permute-start.2
  22.7 0.1 select_reduce_fusion.1
  22.9 0.1 dynamic_slice.9
  23.0 0.1 select_reduce_fusion.2
  23.1 3.1 %collective-permute-done.1 = f32[35,8,128]{2,1,0:T(8,128)S(1)} collective-permute-done((f32[35,8,128]{2,1,0:T(8,128)S(1)}, f32[35,8,128]{2,1,0:T(8,128)S(1)}, u32[]{:S(2)}, u32[]{:S(2)}) %collective-permute-start.1) | collective-permute-done | bytes 143392 | tf_op jit(solution)/shard_map/ppermute | solution.py:265
  26.2 2.5 %collective-permute-done.2 = f32[35,8,128]{2,1,0:T(8,128)S(1)} collective-permute-done((f32[35,8,128]{2,1,0:T(8,128)S(1)}, f32[35,8,128]{2,1,0:T(8,128)S(1)}, u32[]{:S(2)}, u32[]{:S(2)}) %collective-permute-start.2) | collective-permute-done | bytes 143392 | tf_op jit(solution)/shard_map/ppermute | solution.py:265
  28.7 5.5 %collective-permute-start.21 = (f32[17,8,128]{2,1,0:T(8,128)S(1)}, f32[17,8,128]{2,1,0:T(8,128)S(1)}, u32[]{:S(2)}, u32[]{:S(2)}) collective-permute-start(f32[17,8,128]{2,1,0:T(8,128)S(1)} %get-tuple-element.41), channel_id=1, source_target_pairs={{0,56},{8,0},{16,8},{24,16},{32,24},{40,32},{48,40},{56,48},{64,12... | collective-permute-start | bytes 208904 | tf_op jit(solution)/shard_map/ppermute | solution.py:30
  34.2 1.2 %collective-permute-start.19 = (f32[17,8,128]{2,1,0:T(8,128)S(1)}, f32[17,8,128]{2,1,0:T(8,128)S(1)}, u32[]{:S(2)}, u32[]{:S(2)}) collective-permute-start(f32[17,8,128]{2,1,0:T(8,128)S(1)} %get-tuple-element.41), channel_id=1, source_target_pairs={{0,48},{8,56},{16,0},{24,8},{32,16},{40,24},{48,32},{56,40},{64,11... | collective-permute-start | bytes 208904 | tf_op jit(solution)/shard_map/ppermute | solution.py:30
  35.4 1.2 %collective-permute-start.16 = (f32[17,8,128]{2,1,0:T(8,128)S(1)}, f32[17,8,128]{2,1,0:T(8,128)S(1)}, u32[]{:S(2)}, u32[]{:S(2)}) collective-permute-start(f32[17,8,128]{2,1,0:T(8,128)S(1)} %get-tuple-element.41), channel_id=1, source_target_pairs={{0,16},{8,24},{16,32},{24,40},{32,48},{40,56},{48,0},{56,8},{64,80... | collective-permute-start | bytes 208904 | tf_op jit(solution)/shard_map/ppermute | solution.py:30
  36.6 2.8 %collective-permute-start.6 = (f32[18,8,128]{2,1,0:T(8,128)S(1)}, f32[18,8,128]{2,1,0:T(8,128)S(1)}, u32[]{:S(2)}, u32[]{:S(2)}) collective-permute-start(f32[18,8,128]{2,1,0:T(8,128)S(1)} %slice_add_fusion.4), channel_id=1, source_target_pairs={{0,192},{8,200},{16,208},{24,216},{32,224},{40,232},{48,240},{56,2... | collective-permute-start | bytes 221192 | tf_op jit(solution)/shard_map/ppermute | solution.py:30
  39.4 2.3 %collective-permute-done.15 = f32[17,8,128]{2,1,0:T(8,128)S(1)} collective-permute-done((f32[17,8,128]{2,1,0:T(8,128)S(1)}, f32[17,8,128]{2,1,0:T(8,128)S(1)}, u32[]{:S(2)}, u32[]{:S(2)}) %collective-permute-start.15) | collective-permute-done | bytes 69664 | tf_op jit(solution)/shard_map/ppermute | solution.py:30
  41.7 2.9 %collective-permute-start.5 = (f32[18,8,128]{2,1,0:T(8,128)S(1)}, f32[18,8,128]{2,1,0:T(8,128)S(1)}, u32[]{:S(2)}, u32[]{:S(2)}) collective-permute-start(f32[18,8,128]{2,1,0:T(8,128)S(1)} %slice_add_fusion.4), channel_id=1, source_target_pairs={{0,128},{8,136},{16,144},{24,152},{32,160},{40,168},{48,176},{56,1... | collective-permute-start | bytes 221192 | tf_op jit(solution)/shard_map/ppermute | solution.py:30
  44.7 0.5 collective-permute-start.4
  45.1 0.0 collective-permute-done.19
  45.1 0.1 collective-permute-start.18
  45.3 0.3 collective-permute-start.17
  45.5 0.9 collective-permute-done.5
  46.4 1.7 %collective-permute-start.20 = (f32[17,8,128]{2,1,0:T(8,128)S(1)}, f32[17,8,128]{2,1,0:T(8,128)S(1)}, u32[]{:S(2)}, u32[]{:S(2)}) collective-permute-start(f32[17,8,128]{2,1,0:T(8,128)S(1)} %collective-permute-done.19), channel_id=1, source_target_pairs={{0,56},{8,0},{16,8},{24,16},{32,24},{40,32},{48,40},{56,48},{64,12... | collective-permute-start | bytes 208904 | tf_op jit(solution)/shard_map/ppermute | solution.py:30
  48.2 1.3 %collective-permute-done.4 = f32[18,8,128]{2,1,0:T(8,128)S(1)} collective-permute-done((f32[18,8,128]{2,1,0:T(8,128)S(1)}, f32[18,8,128]{2,1,0:T(8,128)S(1)}, u32[]{:S(2)}, u32[]{:S(2)}) %collective-permute-start.4) | collective-permute-done | bytes 73760 | tf_op jit(solution)/shard_map/ppermute | solution.py:30
  49.5 1.6 %collective-permute-start.11 = (f32[72,8,128]{2,1,0:T(8,128)S(1)}, f32[72,8,128]{2,1,0:T(8,128)S(1)}, u32[]{:S(2)}, u32[]{:S(2)}) collective-permute-start(f32[72,8,128]{2,1,0:T(8,128)S(1)} %pad_maximum_fusion.refs_0_), channel_id=1, source_target_pairs={{0,56},{8,0},{16,8},{24,16},{32,24},{40,32},{48,40},{56,48},{64,12... | collective-permute-start | bytes 884744 | tf_op jit(solution)/shard_map/ppermute | solution.py:30
  51.2 0.0 copy-start.4
  51.2 2.0 %collective-permute-start.24 = (f32[136,8,128]{2,1,0:T(8,128)S(1)}, f32[136,8,128]{2,1,0:T(8,128)S(1)}, u32[]{:S(2)}, u32[]{:S(2)}) collective-permute-start(f32[136,8,128]{2,1,0:T(8,128)S(1)} %constant_dynamic-update-slice_fusion.refs_9_), channel_id=1, source_target_pairs={{0,192},{8,200},{16,208},{24,216},{32,224},{40,232},{48,240},{56,2... | collective-permute-start | bytes 1671176 | tf_op jit(solution)/shard_map/ppermute | solution.py:30
  53.2 2.7 %collective-permute-done.11.refs_7_ = f32[72,8,128]{2,1,0:T(8,128)S(1)} collective-permute-done((f32[72,8,128]{2,1,0:T(8,128)S(1)}, f32[72,8,128]{2,1,0:T(8,128)S(1)}, u32[]{:S(2)}, u32[]{:S(2)}) %collective-permute-start.11) | collective-permute-done | bytes 294944 | tf_op jit(solution)/shard_map/ppermute | solution.py:30
  55.9 3.4 %collective-permute-start.12 = (f32[72,8,128]{2,1,0:T(8,128)S(1)}, f32[72,8,128]{2,1,0:T(8,128)S(1)}, u32[]{:S(2)}, u32[]{:S(2)}) collective-permute-start(f32[72,8,128]{2,1,0:T(8,128)S(1)} %collective-permute-done.11.refs_7_), channel_id=1, source_target_pairs={{0,56},{8,0},{16,8},{24,16},{32,24},{40,32},{48,40},{56,48},{64,12... | collective-permute-start | bytes 884744 | tf_op jit(solution)/shard_map/ppermute | solution.py:30
  59.4 3.8 %collective-permute-done.12.refs_6_ = f32[72,8,128]{2,1,0:T(8,128)S(1)} collective-permute-done((f32[72,8,128]{2,1,0:T(8,128)S(1)}, f32[72,8,128]{2,1,0:T(8,128)S(1)}, u32[]{:S(2)}, u32[]{:S(2)}) %collective-permute-start.12) | collective-permute-done | bytes 294944 | tf_op jit(solution)/shard_map/ppermute | solution.py:30
  63.1 3.3 %collective-permute-start.13 = (f32[72,8,128]{2,1,0:T(8,128)S(1)}, f32[72,8,128]{2,1,0:T(8,128)S(1)}, u32[]{:S(2)}, u32[]{:S(2)}) collective-permute-start(f32[72,8,128]{2,1,0:T(8,128)S(1)} %collective-permute-done.12.refs_6_), channel_id=1, source_target_pairs={{0,56},{8,0},{16,8},{24,16},{32,24},{40,32},{48,40},{56,48},{64,12... | collective-permute-start | bytes 884744 | tf_op jit(solution)/shard_map/ppermute | solution.py:30
  66.4 0.0 collective-permute-done.8.refs_2_
  66.4 0.8 slice.111
  67.2 1.6 %collective-permute-start.25 = (f32[68,8,128]{2,1,0:T(8,128)}, f32[68,8,128]{2,1,0:T(8,128)}, u32[]{:S(2)}, u32[]{:S(2)}) collective-permute-start(f32[68,8,128]{2,1,0:T(8,128)} %slice.111), channel_id=1, source_target_pairs={{0,192},{8,200},{16,208},{24,216},{32,224},{40,232},{48,240},{56,2... | collective-permute-start | bytes 835592 | tf_op jit(solution)/shard_map/ppermute | solution.py:30
  68.8 0.8 slice.110
  69.6 1.6 %collective-permute-done.13.refs_5_ = f32[72,8,128]{2,1,0:T(8,128)S(1)} collective-permute-done((f32[72,8,128]{2,1,0:T(8,128)S(1)}, f32[72,8,128]{2,1,0:T(8,128)S(1)}, u32[]{:S(2)}, u32[]{:S(2)}) %collective-permute-start.13) | collective-permute-done | bytes 294944 | tf_op jit(solution)/shard_map/ppermute | solution.py:30
  71.2 0.7 slice.105
  71.9 2.0 %collective-permute-start.14 = (f32[36,8,128]{2,1,0:T(8,128)}, f32[36,8,128]{2,1,0:T(8,128)}, u32[]{:S(2)}, u32[]{:S(2)}) collective-permute-start(f32[36,8,128]{2,1,0:T(8,128)} %slice.105), channel_id=1, source_target_pairs={{0,56},{8,0},{16,8},{24,16},{32,24},{40,32},{48,40},{56,48},{64,12... | collective-permute-start | bytes 442376 | tf_op jit(solution)/shard_map/ppermute | solution.py:30
  73.9 0.4 collective-permute-done.9.refs_3_
  74.3 0.7 slice.104
  75.0 0.6 stack.2.meta_ref
  75.7 0.8 collective-permute-done.23.refs_11_
  76.5 1.6 %collective-permute-done.14.refs_8_ = f32[36,8,128]{2,1,0:T(8,128)} collective-permute-done((f32[36,8,128]{2,1,0:T(8,128)}, f32[36,8,128]{2,1,0:T(8,128)}, u32[]{:S(2)}, u32[]{:S(2)}) %collective-permute-start.14) | collective-permute-done | bytes 147488 | tf_op jit(solution)/shard_map/ppermute | solution.py:30
  78.1 4.2 %collective-permute-done.10.refs_4_ = f32[36,8,128]{2,1,0:T(8,128)} collective-permute-done((f32[36,8,128]{2,1,0:T(8,128)}, f32[36,8,128]{2,1,0:T(8,128)}, u32[]{:S(2)}, u32[]{:S(2)}) %collective-permute-start.10) | collective-permute-done | bytes 147488 | tf_op jit(solution)/shard_map/ppermute | solution.py:30
  82.4 4.4 %place.1 = (f32[16,16,128]{2,1,0:T(8,128)}, f32[16,16,128]{2,1,0:T(8,128)}, f32[16,16,128]{2,1,0:T(8,128)}, f32[16,16,128]{2,1,0:T(8,128)}, f32[16,16,128]{2,1,0...) custom-call(s32[1]{0:T(128)} %bitcast.device_ref, ...), custom_call_target="tpu_custom_call" | custom-call | flops 1000000000 | bytes 6000000 | tf_op jit(solution)/shard_map/place/pallas_call | solution.py:308
  86.8 1.1 collective-permute-start.26
  87.8 3.3 %collective-permute-start.27 = (f32[16,16,128]{2,1,0:T(8,128)}, f32[16,16,128]{2,1,0:T(8,128)S(1)}, u32[]{:S(2)}, u32[]{:S(2)}) collective-permute-start(f32[16,16,128]{2,1,0:T(8,128)} %get-tuple-element.23), channel_id=1, source_target_pairs={{0,4},{1,5},{2,6},{3,7},{4,0},{5,1},{6,2},{7,3},{8,12},{9,13},{10,... | collective-permute-start | bytes 393224 | tf_op jit(solution)/shard_map/ppermute | solution.py:321
  91.1 9.4 %collective-permute-start.29 = (f32[16,16,128]{2,1,0:T(8,128)}, f32[16,16,128]{2,1,0:T(8,128)S(1)}, u32[]{:S(2)}, u32[]{:S(2)}) collective-permute-start(f32[16,16,128]{2,1,0:T(8,128)} %get-tuple-element.25), channel_id=1, source_target_pairs={{0,1},{1,0},{2,3},{3,2},{4,5},{5,4},{6,7},{7,6},{8,9},{9,8},{10,11... | collective-permute-start | bytes 393224 | tf_op jit(solution)/shard_map/ppermute | solution.py:321
  100.5 1.6 %collective-permute-start.30 = (f32[16,16,128]{2,1,0:T(8,128)}, f32[16,16,128]{2,1,0:T(8,128)S(1)}, u32[]{:S(2)}, u32[]{:S(2)}) collective-permute-start(f32[16,16,128]{2,1,0:T(8,128)} %get-tuple-element.26), channel_id=1, source_target_pairs={{0,3},{1,2},{2,5},{3,4},{4,7},{5,6},{6,1},{7,0},{8,11},{9,10},{10,... | collective-permute-start | bytes 393224 | tf_op jit(solution)/shard_map/ppermute | solution.py:321
  102.2 0.8 collective-permute-start.31
  103.0 2.8 %collective-permute-start.32 = (f32[16,16,128]{2,1,0:T(8,128)}, f32[16,16,128]{2,1,0:T(8,128)S(1)}, u32[]{:S(2)}, u32[]{:S(2)}) collective-permute-start(f32[16,16,128]{2,1,0:T(8,128)} %get-tuple-element.28), channel_id=1, source_target_pairs={{0,7},{1,6},{2,1},{3,0},{4,3},{5,2},{6,5},{7,4},{8,15},{9,14},{10,... | collective-permute-start | bytes 393224 | tf_op jit(solution)/shard_map/ppermute | solution.py:321
  105.7 1.3 %bitcast_add_fusion = f32[32]{0:T(128)} fusion(f32[8192]{0:T(1024)} %param.12, s32[]{:T(128)S(6)} %select_n.226, f32[8,128]{1,0:T(8,128)} %get-tuple-element.29, s32[]{:T(128)S(6)} %select_n.223, s32[]{:T(128)S(6)} %select_n.225), kind=kLoop, calls=%fused_computation.98 | loop fusion | flops 32 | bytes 396 | tf_op jit(solution)/shard_map/add | solution.py:336
  107.0 3.5 %collective-permute-done.30 = f32[16,16,128]{2,1,0:T(8,128)S(1)} collective-permute-done((f32[16,16,128]{2,1,0:T(8,128)}, f32[16,16,128]{2,1,0:T(8,128)S(1)}, u32[]{:S(2)}, u32[]{:S(2)}) %collective-permute-start.30) | collective-permute-done | bytes 131104 | tf_op jit(solution)/shard_map/ppermute | solution.py:321
  110.5 0.2 collective-permute-done.32
  110.8 0.4 copy-done.15
  111.2 0.1 copy-done.16
  111.2 0.2 copy-done.17
  111.4 2.9 %finish.1 = f32[1,512,512]{2,1,0:T(8,128)} custom-call(s32[1]{0:T(128)} %bitcast.device_ref, s32[256]{0:T(256)} %owner_ref, f32[256,128]{1,0:T(8,128)} %bitcast.33, f32[256,128]{1,0:T(8,128)} %bitcast.34, f32[256,128]{1,0:T(8,128)} %bitcast.35, f32[256,128]{1,0:T(8,128)} %bitcast.36, f32[256,128]{1,0:T(8,128)} %bitcast.37, f32[256,128]{1,0:T(8,128)} %bitcast.38, ...), custom_call_target="tpu_custom_call" | custom-call | flops 1000000 | bytes 2000000 | tf_op jit(solution)/shard_map/finish/pallas_call | solution.py:323
  (78 shorter events, 0.3 us)
Async XLA Ops:
  0.6 19.1 %copy-start.3 = (s32[256,256]{1,0:T(8,128)S(1)}, s32[256,256]{1,0:T(8,128)}, u32[]{:S(2)}) copy-start(s32[256,256]{1,0:T(8,128)} %index_ref.1) | copy-start | bytes 786436
  0.6 22.3 %copy-start.18 = (s32[256]{0:T(256)S(1)}, s32[256]{0:T(256)}, u32[]{:S(2)}) copy-start(s32[256]{0:T(256)} %owner_ref) | copy-start | bytes 3076
  13.5 5.0 %collective-permute-start = (f32[4,35,8,128]{3,2,1,0:T(8,128)}, f32[4,35,8,128]{3,2,1,0:T(8,128)S(1)}, u32[]{:S(2)}, u32[]{:S(2)}) collective-permute-start(f32[4,35,8,128]{3,2,1,0:T(8,128)} %get-tuple-element.17), channel_id=1, source_target_pairs={{0,1},{1,0},{2,3},{3,2},{4,5},{5,4},{6,7},{7,6},{8,9},{9,8},{10,11... | collective-permute-start | bytes 1720328 | tf_op jit(solution)/shard_map/ppermute | solution.py:262
  20.0 6.2 %collective-permute-start.1 = (f32[35,8,128]{2,1,0:T(8,128)S(1)}, f32[35,8,128]{2,1,0:T(8,128)S(1)}, u32[]{:S(2)}, u32[]{:S(2)}) collective-permute-start(f32[35,8,128]{2,1,0:T(8,128)S(1)} %get-tuple-element.20), channel_id=1, source_target_pairs={{0,2},{1,3},{2,4},{3,5},{4,6},{5,7},{6,0},{7,1},{8,10},{9,11},{10,... | collective-permute-start | bytes 430088 | tf_op jit(solution)/shard_map/ppermute | solution.py:265
  20.1 6.1 %collective-permute-start.3 = (f32[35,8,128]{2,1,0:T(8,128)S(1)}, f32[35,8,128]{2,1,0:T(8,128)S(1)}, u32[]{:S(2)}, u32[]{:S(2)}) collective-permute-start(f32[35,8,128]{2,1,0:T(8,128)S(1)} %get-tuple-element.49), channel_id=1, source_target_pairs={{0,6},{1,7},{2,0},{3,1},{4,2},{5,3},{6,4},{7,5},{8,14},{9,15},{10,... | collective-permute-start | bytes 430088 | tf_op jit(solution)/shard_map/ppermute | solution.py:265
  22.7 6.0 %collective-permute-start.2 = (f32[35,8,128]{2,1,0:T(8,128)S(1)}, f32[35,8,128]{2,1,0:T(8,128)S(1)}, u32[]{:S(2)}, u32[]{:S(2)}) collective-permute-start(f32[35,8,128]{2,1,0:T(8,128)S(1)} %get-tuple-element.50), channel_id=1, source_target_pairs={{0,4},{1,5},{2,6},{3,7},{4,0},{5,1},{6,2},{7,3},{8,12},{9,13},{10,... | collective-permute-start | bytes 430088 | tf_op jit(solution)/shard_map/ppermute | solution.py:265
  28.7 22.4 %collective-permute-start.21 = (f32[17,8,128]{2,1,0:T(8,128)S(1)}, f32[17,8,128]{2,1,0:T(8,128)S(1)}, u32[]{:S(2)}, u32[]{:S(2)}) collective-permute-start(f32[17,8,128]{2,1,0:T(8,128)S(1)} %get-tuple-element.41), channel_id=1, source_target_pairs={{0,56},{8,0},{16,8},{24,16},{32,24},{40,32},{48,40},{56,48},{64,12... | collective-permute-start | bytes 208904 | tf_op jit(solution)/shard_map/ppermute | solution.py:30
  34.2 10.9 %collective-permute-start.19 = (f32[17,8,128]{2,1,0:T(8,128)S(1)}, f32[17,8,128]{2,1,0:T(8,128)S(1)}, u32[]{:S(2)}, u32[]{:S(2)}) collective-permute-start(f32[17,8,128]{2,1,0:T(8,128)S(1)} %get-tuple-element.41), channel_id=1, source_target_pairs={{0,48},{8,56},{16,0},{24,8},{32,16},{40,24},{48,32},{56,40},{64,11... | collective-permute-start | bytes 208904 | tf_op jit(solution)/shard_map/ppermute | solution.py:30
  35.4 9.2 %collective-permute-start.16 = (f32[17,8,128]{2,1,0:T(8,128)S(1)}, f32[17,8,128]{2,1,0:T(8,128)S(1)}, u32[]{:S(2)}, u32[]{:S(2)}) collective-permute-start(f32[17,8,128]{2,1,0:T(8,128)S(1)} %get-tuple-element.41), channel_id=1, source_target_pairs={{0,16},{8,24},{16,32},{24,40},{32,48},{40,56},{48,0},{56,8},{64,80... | collective-permute-start | bytes 208904 | tf_op jit(solution)/shard_map/ppermute | solution.py:30
  36.6 5.1 %collective-permute-start.15 = (f32[17,8,128]{2,1,0:T(8,128)S(1)}, f32[17,8,128]{2,1,0:T(8,128)S(1)}, u32[]{:S(2)}, u32[]{:S(2)}) collective-permute-start(f32[17,8,128]{2,1,0:T(8,128)S(1)} %get-tuple-element.41), channel_id=1, source_target_pairs={{0,8},{8,16},{16,24},{24,32},{32,40},{40,48},{48,56},{56,0},{64,72... | collective-permute-start | bytes 208904 | tf_op jit(solution)/shard_map/ppermute | solution.py:30
  36.6 8.6 %collective-permute-start.6 = (f32[18,8,128]{2,1,0:T(8,128)S(1)}, f32[18,8,128]{2,1,0:T(8,128)S(1)}, u32[]{:S(2)}, u32[]{:S(2)}) collective-permute-start(f32[18,8,128]{2,1,0:T(8,128)S(1)} %slice_add_fusion.4), channel_id=1, source_target_pairs={{0,192},{8,200},{16,208},{24,216},{32,224},{40,232},{48,240},{56,2... | collective-permute-start | bytes 221192 | tf_op jit(solution)/shard_map/ppermute | solution.py:30
  41.7 4.7 %collective-permute-start.5 = (f32[18,8,128]{2,1,0:T(8,128)S(1)}, f32[18,8,128]{2,1,0:T(8,128)S(1)}, u32[]{:S(2)}, u32[]{:S(2)}) collective-permute-start(f32[18,8,128]{2,1,0:T(8,128)S(1)} %slice_add_fusion.4), channel_id=1, source_target_pairs={{0,128},{8,136},{16,144},{24,152},{32,160},{40,168},{48,176},{56,1... | collective-permute-start | bytes 221192 | tf_op jit(solution)/shard_map/ppermute | solution.py:30
  44.7 4.8 %collective-permute-start.4 = (f32[18,8,128]{2,1,0:T(8,128)S(1)}, f32[18,8,128]{2,1,0:T(8,128)S(1)}, u32[]{:S(2)}, u32[]{:S(2)}) collective-permute-start(f32[18,8,128]{2,1,0:T(8,128)S(1)} %slice_add_fusion.4), channel_id=1, source_target_pairs={{0,64},{8,72},{16,80},{24,88},{32,96},{40,104},{48,112},{56,120},{... | collective-permute-start | bytes 221192 | tf_op jit(solution)/shard_map/ppermute | solution.py:30
  45.1 6.0 %collective-permute-start.18 = (f32[17,8,128]{2,1,0:T(8,128)S(1)}, f32[17,8,128]{2,1,0:T(8,128)S(1)}, u32[]{:S(2)}, u32[]{:S(2)}) collective-permute-start(f32[17,8,128]{2,1,0:T(8,128)S(1)} %collective-permute-done.16), channel_id=1, source_target_pairs={{0,16},{8,24},{16,32},{24,40},{32,48},{40,56},{48,0},{56,8},{64,80... | collective-permute-start | bytes 208904 | tf_op jit(solution)/shard_map/ppermute | solution.py:30
  45.3 5.8 %collective-permute-start.17 = (f32[17,8,128]{2,1,0:T(8,128)S(1)}, f32[17,8,128]{2,1,0:T(8,128)S(1)}, u32[]{:S(2)}, u32[]{:S(2)}) collective-permute-start(f32[17,8,128]{2,1,0:T(8,128)S(1)} %collective-permute-done.16), channel_id=1, source_target_pairs={{0,8},{8,16},{16,24},{24,32},{32,40},{40,48},{48,56},{56,0},{64,72... | collective-permute-start | bytes 208904 | tf_op jit(solution)/shard_map/ppermute | solution.py:30
  46.4 4.7 %collective-permute-start.20 = (f32[17,8,128]{2,1,0:T(8,128)S(1)}, f32[17,8,128]{2,1,0:T(8,128)S(1)}, u32[]{:S(2)}, u32[]{:S(2)}) collective-permute-start(f32[17,8,128]{2,1,0:T(8,128)S(1)} %collective-permute-done.19), channel_id=1, source_target_pairs={{0,56},{8,0},{16,8},{24,16},{32,24},{40,32},{48,40},{56,48},{64,12... | collective-permute-start | bytes 208904 | tf_op jit(solution)/shard_map/ppermute | solution.py:30
  49.5 32.8 %copy-start.2 = (f32[72,8,128]{2,1,0:T(8,128)}, f32[72,8,128]{2,1,0:T(8,128)S(1)}, u32[]{:S(2)}) copy-start(f32[72,8,128]{2,1,0:T(8,128)S(1)} %pad_maximum_fusion.refs_0_) | copy-start | bytes 884740
  49.5 6.4 %collective-permute-start.11 = (f32[72,8,128]{2,1,0:T(8,128)S(1)}, f32[72,8,128]{2,1,0:T(8,128)S(1)}, u32[]{:S(2)}, u32[]{:S(2)}) collective-permute-start(f32[72,8,128]{2,1,0:T(8,128)S(1)} %pad_maximum_fusion.refs_0_), channel_id=1, source_target_pairs={{0,56},{8,0},{16,8},{24,16},{32,24},{40,32},{48,40},{56,48},{64,12... | collective-permute-start | bytes 884744 | tf_op jit(solution)/shard_map/ppermute | solution.py:30
  51.1 8.2 %collective-permute-start.7 = (f32[72,8,128]{2,1,0:T(8,128)S(1)}, f32[72,8,128]{2,1,0:T(8,128)S(1)}, u32[]{:S(2)}, u32[]{:S(2)}) collective-permute-start(f32[72,8,128]{2,1,0:T(8,128)S(1)} %pad_maximum_fusion.refs_0_), channel_id=1, source_target_pairs={{0,8},{8,16},{16,24},{24,32},{32,40},{40,48},{48,56},{56,0},{64,72... | collective-permute-start | bytes 884744 | tf_op jit(solution)/shard_map/ppermute | solution.py:30
  51.2 31.1 %copy-start.4 = (f32[136,8,128]{2,1,0:T(8,128)}, f32[136,8,128]{2,1,0:T(8,128)S(1)}, u32[]{:S(2)}) copy-start(f32[136,8,128]{2,1,0:T(8,128)S(1)} %constant_dynamic-update-slice_fusion.refs_9_) | copy-start | bytes 1671172
  51.2 15.2 %collective-permute-start.24 = (f32[136,8,128]{2,1,0:T(8,128)S(1)}, f32[136,8,128]{2,1,0:T(8,128)S(1)}, u32[]{:S(2)}, u32[]{:S(2)}) collective-permute-start(f32[136,8,128]{2,1,0:T(8,128)S(1)} %constant_dynamic-update-slice_fusion.refs_9_), channel_id=1, source_target_pairs={{0,192},{8,200},{16,208},{24,216},{32,224},{40,232},{48,240},{56,2... | collective-permute-start | bytes 1671176 | tf_op jit(solution)/shard_map/ppermute | solution.py:30
  53.2 15.6 %collective-permute-start.22 = (f32[136,8,128]{2,1,0:T(8,128)S(1)}, f32[136,8,128]{2,1,0:T(8,128)S(1)}, u32[]{:S(2)}, u32[]{:S(2)}) collective-permute-start(f32[136,8,128]{2,1,0:T(8,128)S(1)} %constant_dynamic-update-slice_fusion.refs_9_), channel_id=1, source_target_pairs={{0,64},{8,72},{16,80},{24,88},{32,96},{40,104},{48,112},{56,120},{... | collective-permute-start | bytes 1671176 | tf_op jit(solution)/shard_map/ppermute | solution.py:30
  55.9 26.4 %copy-start.7 = (f32[72,8,128]{2,1,0:T(8,128)}, f32[72,8,128]{2,1,0:T(8,128)S(1)}, u32[]{:S(2)}) copy-start(f32[72,8,128]{2,1,0:T(8,128)S(1)} %collective-permute-done.11.refs_7_) | copy-start | bytes 884740
  55.9 7.2 %collective-permute-start.12 = (f32[72,8,128]{2,1,0:T(8,128)S(1)}, f32[72,8,128]{2,1,0:T(8,128)S(1)}, u32[]{:S(2)}, u32[]{:S(2)}) collective-permute-start(f32[72,8,128]{2,1,0:T(8,128)S(1)} %collective-permute-done.11.refs_7_), channel_id=1, source_target_pairs={{0,56},{8,0},{16,8},{24,16},{32,24},{40,32},{48,40},{56,48},{64,12... | collective-permute-start | bytes 884744 | tf_op jit(solution)/shard_map/ppermute | solution.py:30
  59.3 23.0 %copy-start.8 = (f32[72,8,128]{2,1,0:T(8,128)}, f32[72,8,128]{2,1,0:T(8,128)S(1)}, u32[]{:S(2)}) copy-start(f32[72,8,128]{2,1,0:T(8,128)S(1)} %collective-permute-done.7.refs_1_) | copy-start | bytes 884740
  59.3 7.1 %collective-permute-start.8 = (f32[72,8,128]{2,1,0:T(8,128)S(1)}, f32[72,8,128]{2,1,0:T(8,128)S(1)}, u32[]{:S(2)}, u32[]{:S(2)}) collective-permute-start(f32[72,8,128]{2,1,0:T(8,128)S(1)} %collective-permute-done.7.refs_1_), channel_id=1, source_target_pairs={{0,8},{8,16},{16,24},{24,32},{32,40},{40,48},{48,56},{56,0},{64,72... | collective-permute-start | bytes 884744 | tf_op jit(solution)/shard_map/ppermute | solution.py:30
  63.1 19.2 %copy-start.9 = (f32[72,8,128]{2,1,0:T(8,128)}, f32[72,8,128]{2,1,0:T(8,128)S(1)}, u32[]{:S(2)}) copy-start(f32[72,8,128]{2,1,0:T(8,128)S(1)} %collective-permute-done.12.refs_6_) | copy-start | bytes 884740
  63.1 8.1 %collective-permute-start.13 = (f32[72,8,128]{2,1,0:T(8,128)S(1)}, f32[72,8,128]{2,1,0:T(8,128)S(1)}, u32[]{:S(2)}, u32[]{:S(2)}) collective-permute-start(f32[72,8,128]{2,1,0:T(8,128)S(1)} %collective-permute-done.12.refs_6_), channel_id=1, source_target_pairs={{0,56},{8,0},{16,8},{24,16},{32,24},{40,32},{48,40},{56,48},{64,12... | collective-permute-start | bytes 884744 | tf_op jit(solution)/shard_map/ppermute | solution.py:30
  66.4 7.9 %copy-start.10 = (f32[72,8,128]{2,1,0:T(8,128)}, f32[72,8,128]{2,1,0:T(8,128)S(1)}, u32[]{:S(2)}) copy-start(f32[72,8,128]{2,1,0:T(8,128)S(1)} %collective-permute-done.8.refs_2_) | copy-start | bytes 884740
  66.4 7.9 %collective-permute-start.9 = (f32[72,8,128]{2,1,0:T(8,128)S(1)}, f32[72,8,128]{2,1,0:T(8,128)S(1)}, u32[]{:S(2)}, u32[]{:S(2)}) collective-permute-start(f32[72,8,128]{2,1,0:T(8,128)S(1)} %collective-permute-done.8.refs_2_), channel_id=1, source_target_pairs={{0,8},{8,16},{16,24},{24,32},{32,40},{40,48},{48,56},{56,0},{64,72... | collective-permute-start | bytes 884744 | tf_op jit(solution)/shard_map/ppermute | solution.py:30
  66.4 15.9 %copy-start = (f32[136,8,128]{2,1,0:T(8,128)}, f32[136,8,128]{2,1,0:T(8,128)S(1)}, u32[]{:S(2)}) copy-start(f32[136,8,128]{2,1,0:T(8,128)S(1)} %collective-permute-done.24.refs_13_) | copy-start | bytes 1671172
  67.2 8.4 %collective-permute-start.25 = (f32[68,8,128]{2,1,0:T(8,128)}, f32[68,8,128]{2,1,0:T(8,128)}, u32[]{:S(2)}, u32[]{:S(2)}) collective-permute-start(f32[68,8,128]{2,1,0:T(8,128)} %slice.111), channel_id=1, source_target_pairs={{0,192},{8,200},{16,208},{24,216},{32,224},{40,232},{48,240},{56,2... | collective-permute-start | bytes 835592 | tf_op jit(solution)/shard_map/ppermute | solution.py:30
  68.8 13.5 %copy-start.1 = (f32[136,8,128]{2,1,0:T(8,128)}, f32[136,8,128]{2,1,0:T(8,128)S(1)}, u32[]{:S(2)}) copy-start(f32[136,8,128]{2,1,0:T(8,128)S(1)} %collective-permute-done.22.refs_10_) | copy-start | bytes 1671172
  69.6 6.9 %collective-permute-start.23 = (f32[68,8,128]{2,1,0:T(8,128)}, f32[68,8,128]{2,1,0:T(8,128)}, u32[]{:S(2)}, u32[]{:S(2)}) collective-permute-start(f32[68,8,128]{2,1,0:T(8,128)} %slice.110), channel_id=1, source_target_pairs={{0,64},{8,72},{16,80},{24,88},{32,96},{40,104},{48,112},{56,120},{... | collective-permute-start | bytes 835592 | tf_op jit(solution)/shard_map/ppermute | solution.py:30
  71.2 11.2 %copy-start.5 = (f32[72,8,128]{2,1,0:T(8,128)}, f32[72,8,128]{2,1,0:T(8,128)S(1)}, u32[]{:S(2)}) copy-start(f32[72,8,128]{2,1,0:T(8,128)S(1)} %collective-permute-done.13.refs_5_) | copy-start | bytes 884740
  71.9 6.2 %collective-permute-start.14 = (f32[36,8,128]{2,1,0:T(8,128)}, f32[36,8,128]{2,1,0:T(8,128)}, u32[]{:S(2)}, u32[]{:S(2)}) collective-permute-start(f32[36,8,128]{2,1,0:T(8,128)} %slice.105), channel_id=1, source_target_pairs={{0,56},{8,0},{16,8},{24,16},{32,24},{40,32},{48,40},{56,48},{64,12... | collective-permute-start | bytes 442376 | tf_op jit(solution)/shard_map/ppermute | solution.py:30
  74.3 8.1 %copy-start.6 = (f32[72,8,128]{2,1,0:T(8,128)}, f32[72,8,128]{2,1,0:T(8,128)S(1)}, u32[]{:S(2)}) copy-start(f32[72,8,128]{2,1,0:T(8,128)S(1)} %collective-permute-done.9.refs_3_) | copy-start | bytes 884740
  75.0 7.3 %collective-permute-start.10 = (f32[36,8,128]{2,1,0:T(8,128)}, f32[36,8,128]{2,1,0:T(8,128)}, u32[]{:S(2)}, u32[]{:S(2)}) collective-permute-start(f32[36,8,128]{2,1,0:T(8,128)} %slice.104), channel_id=1, source_target_pairs={{0,8},{8,16},{16,24},{24,32},{32,40},{40,48},{48,56},{56,0},{64,72... | collective-permute-start | bytes 442376 | tf_op jit(solution)/shard_map/ppermute | solution.py:30
  86.8 15.4 %collective-permute-start.26 = (f32[16,16,128]{2,1,0:T(8,128)}, f32[16,16,128]{2,1,0:T(8,128)S(1)}, u32[]{:S(2)}, u32[]{:S(2)}) collective-permute-start(f32[16,16,128]{2,1,0:T(8,128)} %get-tuple-element.22), channel_id=1, source_target_pairs={{0,2},{1,3},{2,4},{3,5},{4,6},{5,7},{6,0},{7,1},{8,10},{9,11},{10,... | collective-permute-start | bytes 393224 | tf_op jit(solution)/shard_map/ppermute | solution.py:321
  87.8 15.1 %collective-permute-start.27 = (f32[16,16,128]{2,1,0:T(8,128)}, f32[16,16,128]{2,1,0:T(8,128)S(1)}, u32[]{:S(2)}, u32[]{:S(2)}) collective-permute-start(f32[16,16,128]{2,1,0:T(8,128)} %get-tuple-element.23), channel_id=1, source_target_pairs={{0,4},{1,5},{2,6},{3,7},{4,0},{5,1},{6,2},{7,3},{8,12},{9,13},{10,... | collective-permute-start | bytes 393224 | tf_op jit(solution)/shard_map/ppermute | solution.py:321
  91.1 15.9 %collective-permute-start.28 = (f32[16,16,128]{2,1,0:T(8,128)}, f32[16,16,128]{2,1,0:T(8,128)S(1)}, u32[]{:S(2)}, u32[]{:S(2)}) collective-permute-start(f32[16,16,128]{2,1,0:T(8,128)} %get-tuple-element.24), channel_id=1, source_target_pairs={{0,6},{1,7},{2,0},{3,1},{4,2},{5,3},{6,4},{7,5},{8,14},{9,15},{10,... | collective-permute-start | bytes 393224 | tf_op jit(solution)/shard_map/ppermute | solution.py:321
  91.1 15.9 %collective-permute-start.29 = (f32[16,16,128]{2,1,0:T(8,128)}, f32[16,16,128]{2,1,0:T(8,128)S(1)}, u32[]{:S(2)}, u32[]{:S(2)}) collective-permute-start(f32[16,16,128]{2,1,0:T(8,128)} %get-tuple-element.25), channel_id=1, source_target_pairs={{0,1},{1,0},{2,3},{3,2},{4,5},{5,4},{6,7},{7,6},{8,9},{9,8},{10,11... | collective-permute-start | bytes 393224 | tf_op jit(solution)/shard_map/ppermute | solution.py:321
  100.5 10.0 %collective-permute-start.30 = (f32[16,16,128]{2,1,0:T(8,128)}, f32[16,16,128]{2,1,0:T(8,128)S(1)}, u32[]{:S(2)}, u32[]{:S(2)}) collective-permute-start(f32[16,16,128]{2,1,0:T(8,128)} %get-tuple-element.26), channel_id=1, source_target_pairs={{0,3},{1,2},{2,5},{3,4},{4,7},{5,6},{6,1},{7,0},{8,11},{9,10},{10,... | collective-permute-start | bytes 393224 | tf_op jit(solution)/shard_map/ppermute | solution.py:321
  102.2 8.6 %copy-start.11 = (f32[16,16,128]{2,1,0:T(8,128)}, f32[16,16,128]{2,1,0:T(8,128)S(1)}, u32[]{:S(2)}) copy-start(f32[16,16,128]{2,1,0:T(8,128)S(1)} %collective-permute-done.26) | copy-start | bytes 393220
  102.2 8.4 %collective-permute-start.31 = (f32[16,16,128]{2,1,0:T(8,128)}, f32[16,16,128]{2,1,0:T(8,128)S(1)}, u32[]{:S(2)}, u32[]{:S(2)}) collective-permute-start(f32[16,16,128]{2,1,0:T(8,128)} %get-tuple-element.27), channel_id=1, source_target_pairs={{0,5},{1,4},{2,7},{3,6},{4,1},{5,0},{6,3},{7,2},{8,13},{9,12},{10,... | collective-permute-start | bytes 393224 | tf_op jit(solution)/shard_map/ppermute | solution.py:321
  103.0 7.8 %copy-start.12 = (f32[16,16,128]{2,1,0:T(8,128)}, f32[16,16,128]{2,1,0:T(8,128)S(1)}, u32[]{:S(2)}) copy-start(f32[16,16,128]{2,1,0:T(8,128)S(1)} %collective-permute-done.27) | copy-start | bytes 393220
  103.0 7.8 %collective-permute-start.32 = (f32[16,16,128]{2,1,0:T(8,128)}, f32[16,16,128]{2,1,0:T(8,128)S(1)}, u32[]{:S(2)}, u32[]{:S(2)}) collective-permute-start(f32[16,16,128]{2,1,0:T(8,128)} %get-tuple-element.28), channel_id=1, source_target_pairs={{0,7},{1,6},{2,1},{3,0},{4,3},{5,2},{6,5},{7,4},{8,15},{9,14},{10,... | collective-permute-start | bytes 393224 | tf_op jit(solution)/shard_map/ppermute | solution.py:321
  107.0 3.7 %copy-start.13 = (f32[16,16,128]{2,1,0:T(8,128)}, f32[16,16,128]{2,1,0:T(8,128)S(1)}, u32[]{:S(2)}) copy-start(f32[16,16,128]{2,1,0:T(8,128)S(1)} %collective-permute-done.28) | copy-start | bytes 393220
  107.0 3.7 %copy-start.14 = (f32[16,16,128]{2,1,0:T(8,128)}, f32[16,16,128]{2,1,0:T(8,128)S(1)}, u32[]{:S(2)}) copy-start(f32[16,16,128]{2,1,0:T(8,128)S(1)} %collective-permute-done.29) | copy-start | bytes 393220
  110.5 0.7 copy-start.15
  110.5 0.7 copy-start.16
  110.7 0.7 copy-start.17
